TPU v7x, 32 devices: a whole 2x2x4 slice. The times are simulated.
32 devices in a mesh: rows: 8 (over y, x, core), cols: 4 (over z).
Axes of the slice: x: 2, y: 2, z: 4, core: 2. Of those that a mesh axis runs over, the one named last changes fastest.
Arguments:
- raw_panel: float32 [256, 32768], P('cols', 'rows')
- raw_trail: float32 [1024, 32768], P('cols', 'rows')
- panel_shift: int32 [256], P('cols'), may hold values from 0 to 255, as said below
- trail_shift: int32 [1024], P('cols'), may hold values from 0 to 255, as said below
Outputs:
- r_factor: float32 [256, 256], replicated
- coupling: float32 [256, 1024], P(None, 'cols')
- q_panel: float32 [256, 32768], P('cols', 'rows')
- trail_out: float32 [1024, 32768], P('cols', 'rows')
Inputs may be any that keep to these rules, and one draw needn't show every extreme that they name: `panel_shift`: among the 64 panel and 256 trailing PSFs held by one index of cols, at most 40 have the same value of shift // 32, and exactly 40 share some value. `trail_shift`: as for panel_shift, over the same PSFs of one index of cols.
All inputs are finite; a program needn't handle non-finite values.
Results may differ from a plain program's by a relative error of at most 0.0003.
Values sent between devices are 32-bit elements; how exact they have to be, the bound alone decides.
A program may use at most 64 MiB of HBM per device.

v0:
```python
import math

import jax
import jax.numpy as jnp
from jax import lax
from jax.sharding import PartitionSpec as P

BW = 128
HEAVY = 8


def shifted(shard, axis, by):
    count = lax.axis_size(axis)
    return lax.ppermute(shard, axis, [(i, (i + by) % count) for i in range(count)])


def inner_rows(left, right):
    return lax.dot_general(
        left,
        right,
        (((1,), (1,)), ((), ())),
        precision=lax.Precision.HIGHEST,
        preferred_element_type=jnp.float32,
    )


def on_device(raw_panel, raw_trail, panel_shift, trail_shift):
    highest = lax.Precision.HIGHEST
    pcols = raw_panel.shape[0]
    pixels = raw_panel.shape[1]
    blocks = pixels // BW
    row_devices = lax.axis_size("rows")
    my_row = lax.axis_index("rows")
    local_rows = jnp.concatenate([raw_panel, raw_trail], axis=0)
    shifts = jnp.concatenate([panel_shift, trail_shift], axis=0)
    ncolumns = local_rows.shape[0]
    capacity = max(HEAVY, -(-ncolumns // row_devices))
    device_hops = shifts // blocks
    within = shifts % blocks
    positions = jnp.arange(blocks, dtype=jnp.int32)
    source_idx = (positions[None, :] - within[:, None]) % blocks
    block_view = local_rows.reshape(ncolumns, blocks, BW)
    rolled = jnp.take_along_axis(block_view, source_idx[:, :, None], axis=1)
    stays = (positions[None, :] >= within[:, None])[:, :, None]
    resident = jnp.where(stays, rolled, 0.0).reshape(ncolumns, pixels)
    overflow = jnp.where(stays, 0.0, rolled).reshape(ncolumns, pixels)
    column_ids = jnp.arange(ncolumns, dtype=jnp.int32)
    same_hop = device_hops[:, None] == device_hops[None, :]
    earlier = column_ids[None, :] < column_ids[:, None]
    slot_rank = jnp.sum(jnp.where(same_hop & earlier, 1, 0), axis=1).astype(jnp.int32)
    shifted_over = shifted(overflow, "rows", 1)
    target = (my_row + device_hops) % row_devices * capacity + slot_rank
    outgoing = (
        jnp.zeros((row_devices * capacity, pixels), jnp.float32)
        .at[target]
        .set(resident + shifted_over)
    )
    incoming = lax.all_to_all(
        outgoing.reshape(row_devices, capacity, pixels),
        "rows",
        split_axis=0,
        concat_axis=0,
        tiled=True,
    )
    source = (my_row - device_hops) % row_devices * capacity + slot_rank
    registered = incoming.reshape(row_devices * capacity, pixels)[source]
    reg_panel = registered[:pcols]
    reg_trail = registered[pcols:]
    full_panel = lax.all_gather(reg_panel, "cols", axis=0, tiled=True)
    gram_local = inner_rows(full_panel, full_panel)
    cross_local = inner_rows(full_panel, reg_trail)
    gram_total, cross_total = lax.psum((gram_local, cross_local), "rows")
    lower_factor = jnp.linalg.cholesky(gram_total)
    basis_t = lax.linalg.triangular_solve(lower_factor, full_panel, left_side=True, lower=True)
    coupling_part = lax.linalg.triangular_solve(
        lower_factor, cross_total, left_side=True, lower=True
    )
    removed = lax.dot_general(
        coupling_part,
        basis_t,
        (((0,), (0,)), ((), ())),
        precision=highest,
        preferred_element_type=jnp.float32,
    )
    trail_out = reg_trail - removed
    root = math.sqrt(pixels * row_devices)
    own_basis = lax.dynamic_slice_in_dim(basis_t, lax.axis_index("cols") * pcols, pcols, 0)
    return (lower_factor.T / root, coupling_part / root, own_basis * root, trail_out)


def solution(mesh):
    placed = (P("cols", "rows"), P("cols", "rows"), P("cols"), P("cols"))
    return jax.shard_map(
        on_device,
        mesh=mesh,
        in_specs=placed,
        out_specs=(P(), P(None, "cols"), P("cols", "rows"), P("cols", "rows")),
        check_vma=False,
    )
```

profile of v0, /device:TPU:0, one launch (start us, length us, event | category | flops | bytes accessed | tf_op | source)
XLA Modules:
  0.0 560.8 jit_solution(16874229269762979546)
XLA Ops:
  7.2 0.8 add_select_fusion.2
  7.9 0.2 iota_compare_fusion.2
  8.1 0.2 fusion.17
  8.3 0.1 reshape.614
  8.4 2.8 maximum_bitcast_fusion
  11.3 3.3 copy.19
  14.6 148.4 %gather_fusion.1 = f32[10240,128]{1,0:T(8,128)} fusion(f32[320,32,128]{2,1,0:T(8,128)} %bitcast.58, s32[10240]{0:T(1024)S(1)} %reshape.614), kind=kCustom, calls=%fused_computation.1 | custom fusion | bytes 10567680 | tf_op jit(solution)/shard_map/jit(take_along_axis)/gather | solution.py:43
  163.0 6.4 %select_select_fusion.1 = (f32[320,32,128]{2,1,0:T(8,128)}, f32[320,32,128]{2,1,0:T(8,128)S(1)}) fusion(f32[320,32,128]{2,1,0:T(8,128)} %bitcast.63, pred[320,32]{1,0:T(8,128)(4,1)S(1)} %get-tuple-element.47, pred[320,32]{1,0:T(8,128)(4,1)S(1)} %get-tuple-element.46), kind=kLoop, calls=%fused_computation.16 | loop fusion | flops 3932160 | bytes 15749120 | tf_op jit(solution)/shard_map/jit(_where)/select_n | solution.py:45
  169.4 7.2 %copy.27 = f32[40,8,32,128]{3,1,2,0:T(8,128)} copy(f32[40,8,32,128]{3,2,1,0:T(8,128)S(1)} %bitcast.64) | data formatting | bytes 10485760
  176.6 0.9 collective-permute-start
  177.6 0.2 select_reduce_fusion
  177.8 0.1 fusion.35
  177.9 60.3 %collective-permute-done = f32[320,4096]{1,0:T(8,128)} collective-permute-done((f32[320,4096]{1,0:T(8,128)}, f32[320,4096]{1,0:T(8,128)}, u32[]{:S(2)}, u32[]{:S(2)}) %collective-permute-start) | collective-permute-done | bytes 5242912 | tf_op jit(solution)/shard_map/ppermute | solution.py:14
  238.2 12.7 %scatter_custom_fusion = f32[320,4096]{1,0:T(8,128)} fusion(s32[320]{0:T(512)S(1)} %get-tuple-element.25, f32[320,4096]{1,0:T(8,128)} %collective-permute-done, f32[40,8,32,128]{3,2,1,0:T(8,128)} %bitcast.61, f32[]{:T(128)} %constant.152.clone.1), kind=kCustom, calls=%fused_computation.8 | custom fusion | flops 1310720 | bytes 15728644 | tf_op jit(solution)/shard_map/scatter | solution.py:56
  250.9 4.7 all-to-all-start
  255.7 60.3 %all-to-all-done = f32[8,40,4096]{2,1,0:T(8,128)} async-done(((f32[8,40,4096]{2,1,0:T(8,128)}), f32[8,40,4096]{2,1,0:T(8,128)}, u32[]{:S(2)}, u32[]{:S(2)}) %all-to-all-start) | async-done | bytes 5242912 | tf_op jit(solution)/shard_map/all_to_all | solution.py:58
  315.9 10.3 %gather_fusion = f32[320,4096]{1,0:T(8,128)} fusion(f32[320,4096]{1,0:T(8,128)} %bitcast.4, s32[1024]{0:T(1024)S(1)} %pad_clamp_fusion), kind=kCustom, calls=%fused_computation | custom fusion | bytes 10487040 | tf_op jit(solution)/shard_map/gather | solution.py:66
  326.3 2.3 slice.75
  328.6 0.2 all-reduce.4.cloned.1.call-start
  328.8 80.9 %all-gather.2.cloned.1.call-done = f32[256,4096]{1,0:T(8,128)} async-done(((f32[64,4096]{1,0:T(8,128)}), f32[256,4096]{1,0:T(8,128)}) %all-gather.2.cloned.1.call-update) | async-done | bytes 4194320 | tf_op jit(solution)/shard_map/all_gather | solution.py:69
  409.7 7.8 %fusion.2 = f32[256,256]{1,0:T(8,128)} fusion(f32[256,4096]{1,0:T(8,128)} %all-gather.2.cloned.1.call-done, f32[320,4096]{1,0:T(8,128)} %gather_fusion), kind=kOutput, calls=%fused_computation.17 | convolution fusion | flops 3221225472 | bytes 8650752 | tf_op jit(solution)/shard_map/dot_general | solution.py:18
  417.5 4.2 fusion.44
  421.8 53.5 %all-reduce.4.cloned.1.call-done = (f32[256,256]{0,1:T(8,128)}, f32[256,256]{1,0:T(8,128)}) async-done(((f32[256,256]{0,1:T(8,128)}, f32[256,256]{1,0:T(8,128)}), (f32[256,256]{0,1:T(8,128)}, f32[256,256]{1,0:T(8,128)})) %all-reduce.4.cloned.1.call-update) | async-done | bytes 524304 | tf_op jit(solution)/shard_map/psum | solution.py:72
  475.2 1.1 copy.16
  476.3 1.0 fusion.10
  477.3 11.7 %cholesky.50 = f32[128,128]{1,0:T(8,128)S(1)} custom-call(f32[128,128]{1,0:T(8,128)S(1)} %cholesky.118), custom_call_target="Cholesky" | custom-call | tf_op jit(solution)/shard_map/jit(cholesky)/cholesky | solution.py:73
  489.1 10.0 %custom-call.16 = f32[1,128,128]{1,2,0:T(8,128)S(1)} custom-call(f32[1,128,128]{2,1,0:T(8,128)S(1)} %get-tuple-element.45), custom_call_target="InvertDiagBlocksLowerTriangular" | custom-call | tf_op jit(solution)/shard_map/jit(cholesky)/cholesky | solution.py:73
  499.1 0.2 constant_dynamic-update-slice_fusion
  499.3 0.3 convolution_subtract_fusion.3
  499.6 11.7 %cholesky.105 = f32[128,128]{1,0:T(8,128)S(1)} custom-call(f32[128,128]{1,0:T(8,128)S(1)} %convolution_subtract_fusion.3), custom_call_target="Cholesky" | custom-call | tf_op jit(solution)/shard_map/jit(cholesky)/cholesky | solution.py:73
  511.3 0.6 compare_reduce_fusion
  513.3 0.1 triangular_solve.57
  513.4 4.0 while.1
  513.4 0.6 fusion.55
  514.0 1.4 bitcast_dynamic-update-slice_fusion.2
  515.4 0.6 fusion.55
  516.0 1.4 bitcast_dynamic-update-slice_fusion.2
  517.4 19.7 %custom-call.17 = f32[2,128,128]{1,2,0:T(8,128)S(1)} custom-call(f32[2,128,128]{2,1,0:T(8,128)S(1)} %get-tuple-element.11), custom_call_target="InvertDiagBlocksLowerTriangular" | custom-call | tf_op jit(solution)/shard_map/triangular_solve | solution.py:75
  537.1 3.6 fusion.5
  540.8 1.9 convolution_subtract_fusion.1
  542.7 1.9 fusion.29
  544.7 0.3 fusion.24
  545.0 0.3 convolution_subtract_fusion.2
  545.2 0.3 fusion.30
  545.6 0.7 fusion.12
  546.3 5.3 convolution_subtract_fusion
  551.6 1.1 fusion.8
  552.8 0.8 copy.17
  (28 shorter events, 0.3 us)
Async XLA Ops:
  169.4 8.4 %copy-start.3 = (s32[256]{0:T(256)S(1)}, s32[256]{0:T(256)}, u32[]{:S(2)}) copy-start(s32[256]{0:T(256)} %param.7) | copy-start | bytes 3076
  169.4 8.4 %copy-start.4 = (s32[64]{0:T(128)S(1)}, s32[64]{0:T(128)}, u32[]{:S(2)}) copy-start(s32[64]{0:T(128)} %param.6) | copy-start | bytes 772
  176.6 61.5 %collective-permute-start = (f32[320,4096]{1,0:T(8,128)}, f32[320,4096]{1,0:T(8,128)}, u32[]{:S(2)}, u32[]{:S(2)}) collective-permute-start(f32[320,4096]{1,0:T(8,128)} %bitcast.51), channel_id=1, source_target_pairs={{0,4},{4,8},{8,12},{12,16},{16,20},{20,24},{24,28},{28,0},{1,5},{5... | collective-permute-start | bytes 15728648 | tf_op jit(solution)/shard_map/ppermute | solution.py:14
  250.9 65.0 %all-to-all-start = ((f32[8,40,4096]{2,1,0:T(8,128)}), f32[8,40,4096]{2,1,0:T(8,128)}, u32[]{:S(2)}, u32[]{:S(2)}) async-start(f32[8,40,4096]{2,1,0:T(8,128)} %bitcast.62), calls=%async_computation | async-start | bytes 10485760 | tf_op jit(solution)/shard_map/all_to_all | solution.py:58
  255.6 154.1 %all-gather.2.cloned.1.call-start = ((), (), s32[]{:S(2)}) async-start(), calls=%async_computation.1 | async-start | bytes 5242880 | tf_op jit(solution)/shard_map/all_gather | solution.py:69
  328.6 146.7 %all-reduce.4.cloned.1.call-start = ((), (), s32[]{:S(2)}) async-start(), calls=%async_computation.2 | async-start | bytes 1048576 | tf_op jit(solution)/shard_map/psum | solution.py:72
  409.7 7.8 %copy-start = (f32[256,4096]{1,0:T(8,128)S(1)}, f32[256,4096]{1,0:T(8,128)}, u32[]{:S(2)}) copy-start(f32[256,4096]{1,0:T(8,128)} %all-gather.2.cloned.1.call-done) | copy-start | bytes 12582916
  537.1 3.7 copy-start.1
  537.1 9.2 %slice-start = ((s8[5242880]{0:T(1024)(128)(4,1)}), s8[4194304]{0:T(1024)(128)(4,1)S(1)}, s32[]{:S(2)}) async-start(s8[5242880]{0:T(1024)(128)(4,1)} %bitcast.59), calls=%async_computation.3 | async-start | bytes 8388608
  540.7 3.9 copy-start.2
  540.8 5.5 slice-start.1
Sparse Core Ops, SparseCore 0:
  328.7 80.9 all-gather.1
  421.9 53.3 all-reduce.3
where the time goes:
time: 568 us; the launch traced here: 561 us
  waiting for transfers between devices  255 us (45%)
  local copies, waits for them, and re-layouts  178 us (31%)
  other arithmetic  80.2 us (14%)
  matrix products  26.2 us (5%)
  between operations  16 us (3%)
  starting transfers between devices  5.88 us (1%)
    gather x2, local copies, waits for them, and re-layouts, on_device(): rolled = jnp.take_along_axis(block_view, source_idx[:, :, None], axis=1)  148 us
    all_gather x1, waiting for transfers between devices, on_device(): full_panel = lax.all_gather(reg_panel, 'cols', axis=0, tiled=True)  80.9 us
    all_to_all x1, waiting for transfers between devices, on_device(): lax.all_to_all(outgoing.reshape(row_devices, capacity, pixels), 'rows', s...  60.3 us
    ppermute x1, waiting for transfers between devices, shifted(): lax.ppermute(shard, axis, [(i, (i + by) % count) for i in range(count)])  60.3 us
    psum x1, waiting for transfers between devices, on_device(): gram_total, cross_total = lax.psum((gram_local, cross_local), 'rows')  53.5 us
    another operation x6, other arithmetic, on_device(): lower_factor = jnp.linalg.cholesky(gram_total)  34.1 us
    another operation x3, other arithmetic, on_device(): lax.linalg.triangular_solve(lower_factor, cross_total, left_side=True, lo...  19.7 us
    scatter x1, other arithmetic, on_device(): outgoing = jnp.zeros((row_devices * capacity, pixels), jnp.float32).at[ta...  12.7 us
  transfers between devices with their start and end apart: 4, of which 4 were waited for; matrix products, arithmetic and copies ran while one was open for 0% of the time, Pallas kernels for 0%

commit v1 on v0

v1 whole, which is shorter than its diff:
```python
import functools
import math

import jax
import jax.numpy as jnp
from jax import lax
from jax.experimental import pallas as pl
from jax.experimental.pallas import tpu as pltpu
from jax.sharding import PartitionSpec as P

BW = 128


def roll_kernel(n, count, blocks, shift_ref, in_hbm, out_ref, ring, sems):
    copies = []
    for i in range(n + 1):
        copies.append(
            pltpu.make_async_copy(
                in_hbm.at[i % n], ring.at[:, pl.ds(i * blocks, blocks)], sems.at[i]
            )
        )
    for copy in copies:
        copy.start()
    for copy in copies:
        copy.wait()
    total = n * blocks

    def one(k, carry):
        shift = shift_ref[k]
        for j in range(n):
            start = lax.rem(j * blocks - shift + total, total)
            out_ref[j, k] = ring[k, pl.ds(start, blocks), :]
        return carry

    lax.fori_loop(0, count, one, 0)


def roll_rows(whole, shifts):
    n, count, blocks, _ = whole.shape
    return pl.pallas_call(
        functools.partial(roll_kernel, n, count, blocks),
        out_shape=jax.ShapeDtypeStruct(whole.shape, whole.dtype),
        in_specs=[
            pl.BlockSpec(memory_space=pltpu.SMEM),
            pl.BlockSpec(memory_space=pl.ANY),
        ],
        out_specs=pl.BlockSpec(memory_space=pltpu.VMEM),
        scratch_shapes=[
            pltpu.VMEM((count, (n + 1) * blocks, BW), jnp.float32),
            pltpu.SemaphoreType.DMA((n + 1,)),
        ],
        cost_estimate=pl.CostEstimate(
            flops=0, bytes_accessed=2 * whole.size * 4, transcendentals=0
        ),
    )(shifts, whole)


def register(raw, shifts, n, my_row):
    rows, pixels = raw.shape
    blocks = pixels // BW
    padded = -(-rows // n) * n
    if padded != rows:
        raw = jnp.pad(raw, ((0, padded - rows), (0, 0)))
        shifts = jnp.pad(shifts, (0, padded - rows))
    count = padded // n
    outgoing = raw.reshape(n, count, blocks, BW)
    whole = lax.all_to_all(outgoing, "rows", split_axis=0, concat_axis=0, tiled=True)
    mine = lax.dynamic_slice_in_dim(shifts, my_row * count, count, 0)
    moved = roll_rows(whole, mine)
    back = lax.all_to_all(moved, "rows", split_axis=0, concat_axis=0, tiled=True)
    return back.reshape(padded, pixels)[:rows]


def inner_rows(left, right, precision):
    return lax.dot_general(
        left,
        right,
        (((1,), (1,)), ((), ())),
        precision=precision,
        preferred_element_type=jnp.float32,
    )


def on_device(raw_panel, raw_trail, panel_shift, trail_shift):
    pcols = raw_panel.shape[0]
    pixels = raw_panel.shape[1]
    n = lax.axis_size("rows")
    my_row = lax.axis_index("rows")
    reg_panel = register(raw_panel, panel_shift, n, my_row)
    reg_trail = register(raw_trail, trail_shift, n, my_row)
    full_panel = lax.all_gather(reg_panel, "cols", axis=0, tiled=True)
    gram = lax.psum(inner_rows(full_panel, full_panel, lax.Precision.HIGHEST), "rows")
    lower = jnp.linalg.cholesky(gram)
    eye = jnp.eye(lower.shape[0], dtype=jnp.float32)
    inverse = lax.linalg.triangular_solve(lower, eye, left_side=True, lower=True)
    basis_t = jnp.dot(
        inverse, full_panel, precision=lax.Precision.HIGH, preferred_element_type=jnp.float32
    )
    coupling = lax.psum(inner_rows(basis_t, reg_trail, lax.Precision.HIGH), "rows")
    removed = lax.dot_general(
        coupling,
        basis_t,
        (((0,), (0,)), ((), ())),
        precision=lax.Precision.HIGH,
        preferred_element_type=jnp.float32,
    )
    trail_out = reg_trail - removed
    root = math.sqrt(pixels * n)
    own_basis = lax.dynamic_slice_in_dim(basis_t, lax.axis_index("cols") * pcols, pcols, 0)
    return (lower.T / root, coupling / root, own_basis * root, trail_out)


def solution(mesh):
    placed = (P("cols", "rows"), P("cols", "rows"), P("cols"), P("cols"))
    return jax.shard_map(
        on_device,
        mesh=mesh,
        in_specs=placed,
        out_specs=(P(), P(None, "cols"), P("cols", "rows"), P("cols", "rows")),
        check_vma=False,
    )
```

time: 568 us -> 353 us (0.62); the launches traced: 561 us -> 352 us
  local copies, waits for them, and re-layouts: 178 us -> 17 us
  waiting for transfers between devices: 255 us -> 186 us
  other arithmetic: 80.2 us -> 57.9 us
  blocking collectives: 0 us -> 18.8 us
  Pallas kernels: 0 us -> 9.05 us
  starting transfers between devices: 5.88 us -> 14.9 us
  matrix products: 26.2 us -> 33.4 us
    gather x3 -> x0, local copies, waits for them, and re-layouts: 159 us -> none  [the longest x2 148 us: on_device(): rolled = jnp.take_along_axis(block_view, source_idx[:, :, None], axis=1)]
    all_gather x1, waiting for transfers between devices: 80.9 us -> 10.9 us  [on_device(): full_panel = lax.all_gather(reg_panel, 'cols', axis=0, tiled=True)]
    ppermute x1 -> x0, waiting for transfers between devices: 60.3 us -> none  [shifted(): lax.ppermute(shard, axis, [(i, (i + by) % count) for i in range(count)])]
    psum x1 -> x2, waiting for transfers between devices: 53.5 us -> 112 us  [the longest x1 61.5 us: on_device(): lax.psum(inner_rows(full_panel, full_panel, lax.Precision.HIGHEST), 'rows')]
    all_to_all x0 -> x1, blocking collectives: none -> 18.8 us  [register(): lax.all_to_all(moved, 'rows', split_axis=0, concat_axis=0, tiled=True)]
    dot_general x3 -> x4, matrix products: 17.4 us -> 32.1 us  [the longest x2 16.1 us: inner_rows(): lax.dot_general(left, right, (((1,), (1,)), ((), ())), precision=precisio...]
    scatter x1 -> x0, other arithmetic: 12.7 us -> none  [on_device(): outgoing = jnp.zeros((row_devices * capacity, pixels), jnp.float32).at[ta...]
    all_to_all x1 -> x3, starting transfers between devices: 4.69 us -> 14.6 us  [the longest x2 9.97 us: register(): lax.all_to_all(outgoing, 'rows', split_axis=0, concat_axis=0, tiled=True)]
  transfers between devices with their start and end apart: 4 -> 6, of which waited for: 4 -> 5; matrix products, arithmetic and copies ran while one was open for 0% -> 24% of each run, Pallas kernels for 0% -> 2%
where the time goes in v1:
time: 353 us; the launch traced here: 352 us
  waiting for transfers between devices  186 us (53%)
  other arithmetic  57.9 us (16%)
  matrix products  33.4 us (9%)
  blocking collectives  18.8 us (5%)
  local copies, waits for them, and re-layouts  17 us (5%)
  between operations  15.2 us (4%)
  starting transfers between devices  14.9 us (4%)
  Pallas kernels  9.05 us (3%)
    all_to_all x2, waiting for transfers between devices, register(): lax.all_to_all(outgoing, 'rows', split_axis=0, concat_axis=0, tiled=True)  63.2 us
    psum x1, waiting for transfers between devices, on_device(): lax.psum(inner_rows(full_panel, full_panel, lax.Precision.HIGHEST), 'rows')  61.5 us
    psum x1, waiting for transfers between devices, on_device(): lax.psum(inner_rows(basis_t, reg_trail, lax.Precision.HIGH), 'rows')  50.3 us
    another operation x6, other arithmetic, on_device(): lower = jnp.linalg.cholesky(gram)  34 us
    another operation x3, other arithmetic, on_device(): lax.linalg.triangular_solve(lower, eye, left_side=True, lower=True)  19.9 us
    all_to_all x1, blocking collectives, register(): lax.all_to_all(moved, 'rows', split_axis=0, concat_axis=0, tiled=True)  18.8 us
    dot_general x2, matrix products, inner_rows(): lax.dot_general(left, right, (((1,), (1,)), ((), ())), precision=precisio...  16.1 us
    all_gather x1, waiting for transfers between devices, on_device(): full_panel = lax.all_gather(reg_panel, 'cols', axis=0, tiled=True)  10.9 us
  transfers between devices with their start and end apart: 6, of which 5 were waited for; matrix products, arithmetic and copies ran while one was open for 24% of the time, Pallas kernels for 2%

profile of v1, /device:TPU:0, one launch (start us, length us, event | category | flops | bytes accessed | tf_op | source)
XLA Modules:
  0.0 352.4 jit_solution(17742087743522694233)
XLA Ops:
  7.2 2.4 copy.24
  9.6 5.2 %all-to-all-start = ((f32[8,8,32,128]{3,2,1,0:T(8,128)}), f32[8,8,32,128]{3,2,1,0:T(8,128)S(1)}, u32[]{:S(2)}, u32[]{:S(2)}) async-start(f32[8,8,32,128]{3,2,1,0:T(8,128)} %bitcast.51), calls=%async_computation | async-start | bytes 2097152 | tf_op jit(solution)/shard_map/all_to_all | solution.py:67
  14.8 0.0 all-gather.2.cloned.1.call-start
  14.8 0.6 dynamic_slice.9.shift_ref
  15.4 14.7 %all-to-all-done.in_hbm = f32[8,8,32,128]{3,2,1,0:T(8,128)S(1)} async-done(((f32[8,8,32,128]{3,2,1,0:T(8,128)}), f32[8,8,32,128]{3,2,1,0:T(8,128)S(1)}, u32[]{:S(2)}, u32[]{:S(2)}) %all-to-all-start) | async-done | bytes 1048608 | tf_op jit(solution)/shard_map/all_to_all | solution.py:67
  30.1 1.0 copy-done
  31.1 3.2 shard_map.75
  34.3 18.8 %all_to_all.20 = f32[8,8,32,128]{3,2,1,0:T(8,128)S(1)} all-to-all(f32[8,8,32,128]{3,2,1,0:T(8,128)} %shard_map.75), channel_id=1, replica_groups=mesh['rows'=8,'cols'=4] {'rows'}, dimensions={0} | all-to-all | bytes 2097152 | tf_op jit(solution)/shard_map/all_to_all | solution.py:70
  53.1 1.6 copy.23
  54.7 0.0 all-gather.2.cloned.1.call-update
  54.7 5.0 %copy.14 = f32[32,8,32,128]{3,2,1,0:T(8,128)} copy(f32[32,8,32,128]{3,1,2,0:T(8,128)} %bitcast.59) | data formatting | bytes 8388608
  59.7 4.8 %all-to-all-start.2 = ((f32[8,32,32,128]{3,2,1,0:T(8,128)}), f32[8,32,32,128]{3,2,1,0:T(8,128)}, u32[]{:S(2)}, u32[]{:S(2)}) async-start(f32[8,32,32,128]{3,2,1,0:T(8,128)} %bitcast.58), calls=%async_computation.2 | async-start | bytes 8388608 | tf_op jit(solution)/shard_map/all_to_all | solution.py:67
  64.5 0.6 dynamic_slice.10.shift_ref
  65.1 48.5 %all-to-all-done.2.in_hbm = f32[8,32,32,128]{3,2,1,0:T(8,128)} async-done(((f32[8,32,32,128]{3,2,1,0:T(8,128)}), f32[8,32,32,128]{3,2,1,0:T(8,128)}, u32[]{:S(2)}, u32[]{:S(2)}) %all-to-all-start.2) | async-done | bytes 4194336 | tf_op jit(solution)/shard_map/all_to_all | solution.py:67
  113.6 5.8 %shard_map.76 = f32[8,32,32,128]{3,2,1,0:T(8,128)} custom-call(s32[32]{0:T(128)} %dynamic_slice.10.shift_ref, f32[8,32,32,128]{3,2,1,0:T(8,128)} %all-to-all-done.2.in_hbm), custom_call_target="tpu_custom_call" | custom-call | bytes 8388608 | tf_op jit(solution)/shard_map/pallas_call | solution.py:40
  119.4 4.6 %all-to-all-start.3 = ((f32[8,32,32,128]{3,2,1,0:T(8,128)}), f32[8,32,32,128]{3,2,1,0:T(8,128)}, u32[]{:S(2)}, u32[]{:S(2)}) async-start(f32[8,32,32,128]{3,2,1,0:T(8,128)} %shard_map.76), calls=%async_computation.3 | async-start | bytes 8388608 | tf_op jit(solution)/shard_map/all_to_all | solution.py:70
  124.0 0.0 all-reduce.4.cloned.1.call-start
  124.1 10.9 %all-gather.2.cloned.1.call-done = f32[256,4096]{1,0:T(8,128)} async-done(((f32[64,4096]{1,0:T(8,128)}), f32[256,4096]{1,0:T(8,128)}) %all-gather.2.cloned.1.call-update) | async-done | bytes 4194320 | tf_op jit(solution)/shard_map/all_gather | solution.py:91
  135.0 7.7 %fusion.18 = f32[256,256]{0,1:T(8,128)} fusion(f32[256,4096]{1,0:T(8,128)} %all-gather.2.cloned.1.call-done), kind=kOutput, calls=%fused_computation.44 | convolution fusion | flops 3221225472 | bytes 4456448 | tf_op jit(solution)/shard_map/dot_general | solution.py:75
  142.7 0.0 all-reduce.4.cloned.1.call-update
  142.7 0.2 all-reduce.6.cloned.1.call-start
  143.0 61.5 %all-reduce.4.cloned.1.call-done = f32[256,256]{0,1:T(8,128)} async-done(((f32[256,256]{0,1:T(8,128)}), f32[256,256]{0,1:T(8,128)}) %all-reduce.4.cloned.1.call-update) | async-done | bytes 262160 | tf_op jit(solution)/shard_map/psum | solution.py:92
  204.5 1.1 copy.9
  205.5 1.0 fusion.7
  206.6 11.7 %cholesky.50 = f32[128,128]{1,0:T(8,128)S(1)} custom-call(f32[128,128]{1,0:T(8,128)S(1)} %cholesky.118), custom_call_target="Cholesky" | custom-call | tf_op jit(solution)/shard_map/jit(cholesky)/cholesky | solution.py:93
  218.3 9.8 %custom-call.14 = f32[1,128,128]{1,2,0:T(8,128)S(1)} custom-call(f32[1,128,128]{2,1,0:T(8,128)S(1)} %get-tuple-element.31), custom_call_target="InvertDiagBlocksLowerTriangular" | custom-call | tf_op jit(solution)/shard_map/jit(cholesky)/cholesky | solution.py:93
  228.1 0.2 constant_dynamic-update-slice_fusion.1
  228.4 0.3 convolution_subtract_fusion.2
  228.6 11.7 %cholesky.105 = f32[128,128]{1,0:T(8,128)S(1)} custom-call(f32[128,128]{1,0:T(8,128)S(1)} %convolution_subtract_fusion.2), custom_call_target="Cholesky" | custom-call | tf_op jit(solution)/shard_map/jit(cholesky)/cholesky | solution.py:93
  240.4 0.6 compare_reduce_fusion
  242.4 0.1 triangular_solve.44
  242.4 4.0 %while.1 = (s32[]{:T(128)}, f32[256,256]{1,0:T(8,128)S(1)}, s32[2,2]{1,0:T(2,128)S(1)}, f32[2,128,128]{2,1,0:T(8,128)S(1)}, s32[]{:T(128)}) while((s32[]{:T(128)}, f32[256,256]{1,0:T(8,128)S(1)}, s32[2,2]{1,0:T(2,128)S(1)}, f32[2,128,128]{2,1,0:T(8,128)S(1)}, s32[]{:T(128)}) %tuple.29), condition=%wide.while_cond, body=%wide.while_body.sunk | while | flops 2 | bytes 131181 | solution.py:95
  242.4 0.6 fusion.30
  243.0 1.4 bitcast_dynamic-update-slice_fusion.2
  244.5 0.6 fusion.30
  245.0 1.4 bitcast_dynamic-update-slice_fusion.2
  246.4 19.9 %custom-call.15 = f32[2,128,128]{1,2,0:T(8,128)S(1)} custom-call(f32[2,128,128]{2,1,0:T(8,128)S(1)} %get-tuple-element.11), custom_call_target="InvertDiagBlocksLowerTriangular" | custom-call | tf_op jit(solution)/shard_map/triangular_solve | solution.py:95
  266.3 0.3 fusion.9
  266.6 0.3 convolution_subtract_fusion.1
  266.9 0.3 fusion.12
  267.2 6.2 %fusion.3 = f32[256,4096]{1,0:T(8,128)} fusion(f32[256,4096]{1,0:T(8,128)} %all-gather.2.cloned.1.call-done, f32[128,256]{1,0:T(8,128)S(1)} %fusion.12, f32[128,256]{1,0:T(8,128)S(1)} %fusion.9), kind=kOutput, calls=%fused_computation.11 | convolution fusion | flops 1610678272 | bytes 8650752 | tf_op jit(solution)/shard_map/dot_general | solution.py:96
  273.4 8.4 %fusion = f32[256,256]{1,0:T(8,128)} fusion(f32[256,4096]{1,0:T(8,128)} %fusion.3, f32[32,8,32,128]{3,2,1,0:T(8,128)} %bitcast.19), kind=kOutput, calls=%fused_computation.3 | convolution fusion | flops 1610612736 | bytes 8650752 | tf_op jit(solution)/shard_map/dot_general | solution.py:75
  281.8 0.0 all-reduce.6.cloned.1.call-update
  281.8 2.3 dynamic-slice_multiply_fusion
  284.1 0.8 copy.10
  285.0 50.3 %all-reduce.6.cloned.1.call-done = f32[256,256]{1,0:T(8,128)} async-done(((f32[256,256]{1,0:T(8,128)}), f32[256,256]{1,0:T(8,128)}) %all-reduce.6.cloned.1.call-update) | async-done | bytes 262160 | tf_op jit(solution)/shard_map/psum | solution.py:99
  335.3 9.8 %convolution_subtract_fusion = f32[256,4096]{1,0:T(8,128)} fusion(f32[256,256]{1,0:T(8,128)} %all-reduce.6.cloned.1.call-done, f32[256,4096]{1,0:T(8,128)} %fusion.3, f32[32,8,32,128]{3,2,1,0:T(8,128)} %bitcast.19), kind=kOutput, calls=%fused_computation.2 | convolution fusion | flops 1611661312 | bytes 12845056 | tf_op jit(solution)/shard_map/dot_general | solution.py:100
  345.1 0.7 broadcast_multiply_fusion
  (18 shorter events, 0.2 us)
Async XLA Ops:
  7.2 7.6 %copy-start.3 = (s32[64]{0:T(128)S(1)}, s32[64]{0:T(128)}, u32[]{:S(2)}) copy-start(s32[64]{0:T(128)} %param.6) | copy-start | bytes 772
  9.6 20.6 %all-to-all-start = ((f32[8,8,32,128]{3,2,1,0:T(8,128)}), f32[8,8,32,128]{3,2,1,0:T(8,128)S(1)}, u32[]{:S(2)}, u32[]{:S(2)}) async-start(f32[8,8,32,128]{3,2,1,0:T(8,128)} %bitcast.51), calls=%async_computation | async-start | bytes 2097152 | tf_op jit(solution)/shard_map/all_to_all | solution.py:67
  14.8 120.2 %all-gather.2.cloned.1.call-start = ((), (), s32[]{:S(2)}) async-start(), calls=%async_computation.4 | async-start | bytes 5242880 | tf_op jit(solution)/shard_map/all_gather | solution.py:91
  30.1 1.0 copy-start
  59.7 4.8 %copy-start.2 = (s32[256]{0:T(256)S(1)}, s32[256]{0:T(256)}, u32[]{:S(2)}) copy-start(s32[256]{0:T(256)} %param.7) | copy-start | bytes 3076
  59.7 53.9 %all-to-all-start.2 = ((f32[8,32,32,128]{3,2,1,0:T(8,128)}), f32[8,32,32,128]{3,2,1,0:T(8,128)}, u32[]{:S(2)}, u32[]{:S(2)}) async-start(f32[8,32,32,128]{3,2,1,0:T(8,128)} %bitcast.58), calls=%async_computation.2 | async-start | bytes 8388608 | tf_op jit(solution)/shard_map/all_to_all | solution.py:67
  119.4 154.0 %all-to-all-start.3 = ((f32[8,32,32,128]{3,2,1,0:T(8,128)}), f32[8,32,32,128]{3,2,1,0:T(8,128)}, u32[]{:S(2)}, u32[]{:S(2)}) async-start(f32[8,32,32,128]{3,2,1,0:T(8,128)} %shard_map.76), calls=%async_computation.3 | async-start | bytes 8388608 | tf_op jit(solution)/shard_map/all_to_all | solution.py:70
  124.0 80.4 %all-reduce.4.cloned.1.call-start = ((), (), s32[]{:S(2)}) async-start(), calls=%async_computation.5 | async-start | bytes 524288 | tf_op jit(solution)/shard_map/psum | solution.py:92
  142.7 192.6 %all-reduce.6.cloned.1.call-start = ((), (), s32[]{:S(2)}) async-start(), calls=%async_computation.6 | async-start | bytes 524288 | tf_op jit(solution)/shard_map/psum | solution.py:99
  335.3 9.8 %copy-start.1 = (f32[256,256]{1,0:T(8,128)S(1)}, f32[256,256]{1,0:T(8,128)}, u32[]{:S(2)}) copy-start(f32[256,256]{1,0:T(8,128)} %all-reduce.6.cloned.1.call-done) | copy-start | bytes 786436
Sparse Core Ops, SparseCore 0:
  54.9 80.0 all-gather.1
  142.8 61.5 all-reduce.3
  281.9 53.2 all-reduce.5

commit v2 on v1

--- a/solution.py
+++ b/solution.py
@@ -9,6 +9,7 @@
 from jax.sharding import PartitionSpec as P
 
 BW = 128
+MESH = pl.DeviceIdType.MESH
 
 
 def roll_kernel(n, count, blocks, shift_ref, in_hbm, out_ref, ring, sems):
@@ -81,33 +82,171 @@
     )
 
 
+def sum_kernel(n, part_ref, out_ref, landed, send_one, recv_one, send_two, recv_two):
+    me = lax.axis_index("rows")
+    barrier = pltpu.get_barrier_semaphore()
+    for d in range(1, n):
+        pl.semaphore_signal(
+            barrier, inc=1, device_id={"rows": lax.rem(me + d, n)}, device_id_type=MESH
+        )
+    pl.semaphore_wait(barrier, n - 1)
+    scatter = []
+    for d in range(1, n):
+        to = lax.rem(me + d, n)
+        copy = pltpu.make_async_remote_copy(
+            src_ref=part_ref.at[to],
+            dst_ref=landed.at[d - 1],
+            send_sem=send_one.at[d - 1],
+            recv_sem=recv_one.at[d - 1],
+            device_id={"rows": to},
+            device_id_type=MESH,
+        )
+        copy.start()
+        scatter.append(copy)
+    total = part_ref[me]
+    for d in range(1, n):
+        scatter[d - 1].wait_recv()
+        total = total + landed[d - 1]
+    out_ref[me] = total
+    spread = []
+    for d in range(1, n):
+        to = lax.rem(me + d, n)
+        copy = pltpu.make_async_remote_copy(
+            src_ref=out_ref.at[me],
+            dst_ref=out_ref.at[me],
+            send_sem=send_two.at[d - 1],
+            recv_sem=recv_two.at[d - 1],
+            device_id={"rows": to},
+            device_id_type=MESH,
+        )
+        copy.start()
+        spread.append(copy)
+    for copy in scatter:
+        copy.wait_send()
+    for copy in spread:
+        copy.wait_recv()
+    for copy in spread:
+        copy.wait_send()
+
+
+def sum_rows(part, n, ident):
+    rows, columns = part.shape
+    cut = (n, rows // n, columns)
+    out = pl.pallas_call(
+        functools.partial(sum_kernel, n),
+        out_shape=jax.ShapeDtypeStruct(cut, jnp.float32),
+        in_specs=[pl.BlockSpec(memory_space=pltpu.VMEM)],
+        out_specs=pl.BlockSpec(memory_space=pltpu.VMEM),
+        scratch_shapes=[pltpu.VMEM((n - 1,) + cut[1:], jnp.float32)]
+        + [pltpu.SemaphoreType.DMA((n - 1,))] * 4,
+        compiler_params=pltpu.CompilerParams(collective_id=ident, has_side_effects=True),
+        cost_estimate=pl.CostEstimate(
+            flops=0, bytes_accessed=16 * part.size * 4, transcendentals=0
+        ),
+    )(part.reshape(cut))
+    return out.reshape(rows, columns)
+
+
+def factor_kernel(size, tile, scale, gram_ref, upper_ref, inv_ref, aug, pair):
+    grow = lax.broadcasted_iota(jnp.int32, (size, size), 0)
+    gcol = lax.broadcasted_iota(jnp.int32, (size, size), 1)
+    aug[:, 0:size] = gram_ref[...]
+    aug[:, size : 2 * size] = jnp.where(grow == gcol, 1.0, 0.0)
+    row = lax.broadcasted_iota(jnp.int32, (tile, 2 * tile), 0)
+    col = lax.broadcasted_iota(jnp.int32, (tile, 2 * tile), 1)
+    for lo in range(0, size, tile):
+        hi = lo + tile
+        pair[...] = jnp.where(col == row + tile, 1.0, 0.0)
+        pair[:, 0:tile] = aug[lo:hi, lo:hi]
+        w = pair[...]
+        pivots = jnp.zeros((tile, 1), jnp.float32)
+        for j in range(tile):
+            base = j // 8 * 8
+            live = w[base:, :]
+            lead = w[j : j + 1, :]
+            pivot = lead[:, j : j + 1]
+            pivots = jnp.where(row[:, 0:1] == j, pivot, pivots)
+            if j + 1 == tile:
+                break
+            mult = jnp.where(row[base:, 0:1] > j, live[:, j : j + 1], 0.0)
+            live = live - mult * (lead / pivot)
+            w = live if base == 0 else jnp.concatenate([w[:base], live], axis=0)
+        pair[...] = w * (1.0 / jnp.sqrt(pivots))
+        inverse = pair[:, tile : 2 * tile]
+        lead_rows = lax.dot_general(
+            inverse,
+            aug[lo:hi, :],
+            (((1,), (0,)), ((), ())),
+            precision=lax.Precision.HIGHEST,
+            preferred_element_type=jnp.float32,
+        )
+        keep = gcol[lo:hi] >= grow[lo:hi]
+        upper = jnp.where(keep, lead_rows[:, 0:size], 0.0)
+        upper_ref[lo:hi, :] = upper * scale
+        inv_ref[lo:hi, :] = lead_rows[:, size : 2 * size]
+        if hi < size:
+            aug[...] = aug[...] - lax.dot_general(
+                upper,
+                lead_rows,
+                (((0,), (0,)), ((), ())),
+                precision=lax.Precision.HIGHEST,
+                preferred_element_type=jnp.float32,
+            )
+
+
+def factor(gram, scale):
+    size = gram.shape[0]
+    tile = min(64, size)
+    square = jax.ShapeDtypeStruct((size, size), jnp.float32)
+    return pl.pallas_call(
+        functools.partial(factor_kernel, size, tile, scale),
+        out_shape=(square, square),
+        in_specs=[pl.BlockSpec(memory_space=pltpu.VMEM)],
+        out_specs=(pl.BlockSpec(memory_space=pltpu.VMEM),) * 2,
+        scratch_shapes=[
+            pltpu.VMEM((size, 2 * size), jnp.float32),
+            pltpu.VMEM((tile, 2 * tile), jnp.float32),
+        ],
+        cost_estimate=pl.CostEstimate(
+            flops=2 * size**3, bytes_accessed=60 * size * size * 4, transcendentals=0
+        ),
+    )(gram)
+
+
 def on_device(raw_panel, raw_trail, panel_shift, trail_shift):
     pcols = raw_panel.shape[0]
     pixels = raw_panel.shape[1]
     n = lax.axis_size("rows")
     my_row = lax.axis_index("rows")
+    root = math.sqrt(pixels * n)
     reg_panel = register(raw_panel, panel_shift, n, my_row)
     reg_trail = register(raw_trail, trail_shift, n, my_row)
     full_panel = lax.all_gather(reg_panel, "cols", axis=0, tiled=True)
-    gram = lax.psum(inner_rows(full_panel, full_panel, lax.Precision.HIGHEST), "rows")
-    lower = jnp.linalg.cholesky(gram)
-    eye = jnp.eye(lower.shape[0], dtype=jnp.float32)
-    inverse = lax.linalg.triangular_solve(lower, eye, left_side=True, lower=True)
-    basis_t = jnp.dot(
-        inverse, full_panel, precision=lax.Precision.HIGH, preferred_element_type=jnp.float32
-    )
-    coupling = lax.psum(inner_rows(basis_t, reg_trail, lax.Precision.HIGH), "rows")
+    gram = sum_rows(inner_rows(full_panel, full_panel, lax.Precision.HIGHEST), n, 1)
+    r_factor, inverse = factor(gram, 1.0 / root)
+    cross = sum_rows(inner_rows(full_panel, reg_trail, lax.Precision.HIGH), n, 2)
+    highest = lax.Precision.HIGHEST
+    coupling = jnp.dot(inverse, cross, precision=highest, preferred_element_type=jnp.float32)
+    weights = lax.dot_general(
+        inverse,
+        coupling,
+        (((0,), (0,)), ((), ())),
+        precision=highest,
+        preferred_element_type=jnp.float32,
+    )
     removed = lax.dot_general(
-        coupling,
-        basis_t,
+        weights,
+        full_panel,
         (((0,), (0,)), ((), ())),
         precision=lax.Precision.HIGH,
         preferred_element_type=jnp.float32,
     )
     trail_out = reg_trail - removed
-    root = math.sqrt(pixels * n)
-    own_basis = lax.dynamic_slice_in_dim(basis_t, lax.axis_index("cols") * pcols, pcols, 0)
-    return (lower.T / root, coupling / root, own_basis * root, trail_out)
+    own = lax.dynamic_slice_in_dim(inverse, lax.axis_index("cols") * pcols, pcols, 0)
+    q_panel = jnp.dot(
+        own * root, full_panel, precision=lax.Precision.HIGH, preferred_element_type=jnp.float32
+    )
+    return (r_factor, coupling / root, q_panel, trail_out)
 
 
 def solution(mesh):

time: 353 us -> 262 us (0.74)
  waiting for transfers between devices: 186 us -> 121 us
  other arithmetic: 57.9 us -> 0 us
  Pallas kernels: 9.05 us -> 61.7 us
  blocking collectives: 18.8 us -> 0 us
    psum x2 -> x0, waiting for transfers between devices: 112 us -> none  [the longest x1 61.5 us: on_device(): lax.psum(inner_rows(full_panel, full_panel, lax.Precision.HIGHEST), 'rows')]
    all_to_all x1 -> x2, waiting for transfers between devices: 0.01 us -> 59.4 us  [register(): lax.all_to_all(moved, 'rows', split_axis=0, concat_axis=0, tiled=True)]
    another operation x9 -> x0, other arithmetic: 53.9 us -> none  [the longest x6 34 us: on_device(): lower = jnp.linalg.cholesky(gram)]
    pallas_call x0 -> x3, Pallas kernels: none -> 52.6 us  [the longest x1 27.1 us: factor(): pl.pallas_call(functools.partial(factor_kernel, size, tile, scale), out_s...]
    all_to_all x1 -> x0, blocking collectives: 18.8 us -> none  [register(): lax.all_to_all(moved, 'rows', split_axis=0, concat_axis=0, tiled=True)]
    all_gather x1, waiting for transfers between devices: 10.9 us -> 0.01 us  [on_device(): full_panel = lax.all_gather(reg_panel, 'cols', axis=0, tiled=True)]
    reshape x0 -> x1, local copies, waits for them, and re-layouts: none -> 4.94 us  [register(): return back.reshape(padded, pixels)[:rows]]
    another operation x9 -> x0, local copies, waits for them, and re-layouts: 4.05 us -> none
  transfers between devices with their start and end apart: 6 -> 5, of which waited for: 5 -> 4; matrix products, arithmetic and copies ran while one was open for 24% -> 5% of each run, Pallas kernels for 2% -> 2%
where the time goes in v2:
time: 262 us
  waiting for transfers between devices  121 us (46%)
  Pallas kernels  61.7 us (24%)
  matrix products  30.6 us (12%)
  starting transfers between devices  18.1 us (7%)
  local copies, waits for them, and re-layouts  16 us (6%)
  between operations  14.1 us (5%)
    all_to_all x2, waiting for transfers between devices, register(): lax.all_to_all(outgoing, 'rows', split_axis=0, concat_axis=0, tiled=True)  61.6 us
    all_to_all x2, waiting for transfers between devices, register(): lax.all_to_all(moved, 'rows', split_axis=0, concat_axis=0, tiled=True)  59.4 us
    pallas_call x1, Pallas kernels, factor(): pl.pallas_call(functools.partial(factor_kernel, size, tile, scale), out_s...  27.1 us
    pallas_call x2, Pallas kernels, sum_rows(): pl.pallas_call(functools.partial(sum_kernel, n), out_shape=jax.ShapeDtype...  25.5 us
    dot_general x2, matrix products, inner_rows(): lax.dot_general(left, right, (((1,), (1,)), ((), ())), precision=precisio...  13.8 us
    unnamed x13, local copies, waits for them, and re-layouts  9.9 us
    all_to_all x2, starting transfers between devices, register(): lax.all_to_all(outgoing, 'rows', split_axis=0, concat_axis=0, tiled=True)  9.88 us
    pallas_call x2, Pallas kernels, roll_rows(): pl.pallas_call(functools.partial(roll_kernel, n, count, blocks), out_shap...  9.06 us
  transfers between devices with their start and end apart: 5, of which 4 were waited for; matrix products, arithmetic and copies ran while one was open for 5% of the time, Pallas kernels for 2%

profile of v2, /device:TPU:0, one launch (start us, length us, event | category | flops | bytes accessed | tf_op | source)
XLA Modules:
  0.0 261.6 jit_solution(7859511311912323825)
XLA Ops:
  7.2 0.0 copy-start.4
  7.2 2.4 copy.16
  9.6 5.2 %all-to-all-start = ((f32[8,8,32,128]{3,2,1,0:T(8,128)}), f32[8,8,32,128]{3,2,1,0:T(8,128)S(1)}, u32[]{:S(2)}, u32[]{:S(2)}) async-start(f32[8,8,32,128]{3,2,1,0:T(8,128)} %bitcast.33), calls=%async_computation | async-start | bytes 2097152 | tf_op jit(solution)/shard_map/all_to_all | solution.py:68
  14.8 0.0 copy-done.4
  14.8 0.6 dynamic_slice.9.shift_ref
  15.4 14.8 %all-to-all-done.in_hbm = f32[8,8,32,128]{3,2,1,0:T(8,128)S(1)} async-done(((f32[8,8,32,128]{3,2,1,0:T(8,128)}), f32[8,8,32,128]{3,2,1,0:T(8,128)S(1)}, u32[]{:S(2)}, u32[]{:S(2)}) %all-to-all-start) | async-done | bytes 1048608 | tf_op jit(solution)/shard_map/all_to_all | solution.py:68
  30.1 0.0 copy-start.1
  30.1 1.0 copy-done.1
  31.1 3.2 %shard_map.75 = f32[8,8,32,128]{3,2,1,0:T(8,128)} custom-call(s32[8]{0:T(128)} %dynamic_slice.9.shift_ref, f32[8,8,32,128]{3,2,1,0:T(8,128)} %copy-done.1), custom_call_target="tpu_custom_call" | custom-call | bytes 2097152 | tf_op jit(solution)/shard_map/pallas_call | solution.py:41
  34.3 3.6 %all-to-all-start.1 = ((f32[8,8,32,128]{3,2,1,0:T(8,128)}), f32[8,8,32,128]{3,2,1,0:T(8,128)S(1)}, u32[]{:S(2)}, u32[]{:S(2)}) async-start(f32[8,8,32,128]{3,2,1,0:T(8,128)} %shard_map.75), calls=%async_computation.1 | async-start | bytes 2097152 | tf_op jit(solution)/shard_map/all_to_all | solution.py:71
  37.9 5.0 %copy.10 = f32[32,8,32,128]{3,2,1,0:T(8,128)} copy(f32[32,8,32,128]{3,1,2,0:T(8,128)} %bitcast.36) | data formatting | bytes 8388608
  42.9 10.4 %all-to-all-done.1 = f32[8,8,32,128]{3,2,1,0:T(8,128)S(1)} async-done(((f32[8,8,32,128]{3,2,1,0:T(8,128)}), f32[8,8,32,128]{3,2,1,0:T(8,128)S(1)}, u32[]{:S(2)}, u32[]{:S(2)}) %all-to-all-start.1) | async-done | bytes 1048608 | tf_op jit(solution)/shard_map/all_to_all | solution.py:71
  53.2 0.0 copy-start.3
  53.2 4.7 %all-to-all-start.2 = ((f32[8,32,32,128]{3,2,1,0:T(8,128)}), f32[8,32,32,128]{3,2,1,0:T(8,128)}, u32[]{:S(2)}, u32[]{:S(2)}) async-start(f32[8,32,32,128]{3,2,1,0:T(8,128)} %bitcast.35), calls=%async_computation.2 | async-start | bytes 8388608 | tf_op jit(solution)/shard_map/all_to_all | solution.py:68
  57.9 0.0 all-gather.2.cloned.1.call-start
  58.0 1.6 copy.15
  59.6 0.0 all-gather.2.cloned.1.call-update
  59.6 0.0 copy-done.3
  59.6 0.6 dynamic_slice.10.shift_ref
  60.2 46.8 %all-to-all-done.2.in_hbm = f32[8,32,32,128]{3,2,1,0:T(8,128)} async-done(((f32[8,32,32,128]{3,2,1,0:T(8,128)}), f32[8,32,32,128]{3,2,1,0:T(8,128)}, u32[]{:S(2)}, u32[]{:S(2)}) %all-to-all-start.2) | async-done | bytes 4194336 | tf_op jit(solution)/shard_map/all_to_all | solution.py:68
  107.0 5.8 %shard_map.78 = f32[8,32,32,128]{3,2,1,0:T(8,128)} custom-call(s32[32]{0:T(128)} %dynamic_slice.10.shift_ref, f32[8,32,32,128]{3,2,1,0:T(8,128)} %all-to-all-done.2.in_hbm), custom_call_target="tpu_custom_call" | custom-call | bytes 8388608 | tf_op jit(solution)/shard_map/pallas_call | solution.py:41
  112.9 4.6 %all-to-all-start.3 = ((f32[8,32,32,128]{3,2,1,0:T(8,128)}), f32[8,32,32,128]{3,2,1,0:T(8,128)}, u32[]{:S(2)}, u32[]{:S(2)}) async-start(f32[8,32,32,128]{3,2,1,0:T(8,128)} %shard_map.78), calls=%async_computation.3 | async-start | bytes 8388608 | tf_op jit(solution)/shard_map/all_to_all | solution.py:71
  117.4 49.1 %all-to-all-done.3 = f32[8,32,32,128]{3,2,1,0:T(8,128)} async-done(((f32[8,32,32,128]{3,2,1,0:T(8,128)}), f32[8,32,32,128]{3,2,1,0:T(8,128)}, u32[]{:S(2)}, u32[]{:S(2)}) %all-to-all-start.3) | async-done | bytes 4194336 | tf_op jit(solution)/shard_map/all_to_all | solution.py:71
  166.5 4.9 %reshape.38 = f32[256,4096,1]{1,0,2:T(8,128)} reshape(f32[8,32,32,128]{3,2,1,0:T(8,128)} %all-to-all-done.3) | data formatting | bytes 8388608 | tf_op jit(solution)/shard_map/reshape | solution.py:72
  171.5 0.0 all-gather.2.cloned.1.call-done
  171.5 6.1 %fusion.7.part_ref = f32[8,32,256]{2,1,0:T(8,128)} fusion(f32[8,32,4096]{2,1,0:T(8,128)} %bitcast.34, f32[256,4096,1]{1,0,2:T(8,128)} %reshape.38), kind=kOutput, calls=%fused_computation.11 | convolution fusion | flops 1610612736 | bytes 8650752 | tf_op jit(solution)/shard_map/dot_general | solution.py:76
  177.6 12.3 %shard_map.79 = f32[8,32,256]{2,1,0:T(8,128)} custom-call(f32[8,32,256]{2,1,0:T(8,128)} %fusion.7.part_ref), custom_call_target="tpu_custom_call" | custom-call | bytes 4194304 | tf_op jit(solution)/shard_map/pallas_call | solution.py:135
  189.9 0.0 copy-start.2
  189.9 7.7 %fusion.6 = f32[256,256]{1,0:T(8,128)} fusion(f32[256,4096]{1,0:T(8,128)} %all-gather.2.cloned.1.call-done), kind=kOutput, calls=%fused_computation.10 | convolution fusion | flops 3221225472 | bytes 4456448 | tf_op jit(solution)/shard_map/dot_general | solution.py:76
  197.6 13.2 %shard_map.76 = f32[8,32,256]{2,1,0:T(8,128)} custom-call(f32[8,32,256]{2,1,0:T(8,128)} %bitcast.38), custom_call_target="tpu_custom_call" | custom-call | bytes 4194304 | tf_op jit(solution)/shard_map/pallas_call | solution.py:135
  210.8 27.1 %shard_map.77 = (f32[256,256]{1,0:T(8,128)}, f32[256,256]{1,0:T(8,128)}) custom-call(f32[256,256]{1,0:T(8,128)} %bitcast.40), custom_call_target="tpu_custom_call" | custom-call | flops 33554432 | bytes 15728640 | tf_op jit(solution)/shard_map/pallas_call | solution.py:201
  238.0 0.0 copy-start
  238.0 0.0 copy-done.2
  238.0 2.2 broadcast_multiply_fusion
  240.1 1.5 fusion.8
  241.7 4.6 %fusion = f32[64,4096]{1,0:T(8,128)} fusion(f32[256,4096]{1,0:T(8,128)} %all-gather.2.cloned.1.call-done, f32[256,256]{1,0:T(8,128)} %get-tuple-element.7, s32[]{:T(128)S(6)} %select_n.11), kind=kOutput, calls=%fused_computation.4 | convolution fusion | flops 402669568 | bytes 5308420 | tf_op jit(solution)/shard_map/dot_general | solution.py:246
  246.3 0.0 copy-done
  246.3 8.5 %convolution_subtract_fusion = f32[256,4096]{1,0:T(8,128)} fusion(f32[256,256]{1,0:T(8,128)S(1)} %fusion.8, f32[256,4096]{1,0:T(8,128)S(1)} %copy-done, f32[32,8,32,128]{3,2,1,0:T(8,128)} %bitcast.15), kind=kOutput, calls=%fused_computation | convolution fusion | flops 1611661312 | bytes 12845056 | tf_op jit(solution)/shard_map/dot_general | solution.py:237
Async XLA Ops:
  7.2 7.6 %copy-start.4 = (s32[64]{0:T(128)S(1)}, s32[64]{0:T(128)}, u32[]{:S(2)}) copy-start(s32[64]{0:T(128)} %param.6) | copy-start | bytes 772
  9.6 20.6 %all-to-all-start = ((f32[8,8,32,128]{3,2,1,0:T(8,128)}), f32[8,8,32,128]{3,2,1,0:T(8,128)S(1)}, u32[]{:S(2)}, u32[]{:S(2)}) async-start(f32[8,8,32,128]{3,2,1,0:T(8,128)} %bitcast.33), calls=%async_computation | async-start | bytes 2097152 | tf_op jit(solution)/shard_map/all_to_all | solution.py:68
  30.1 1.0 copy-start.1
  34.3 18.9 %all-to-all-start.1 = ((f32[8,8,32,128]{3,2,1,0:T(8,128)}), f32[8,8,32,128]{3,2,1,0:T(8,128)S(1)}, u32[]{:S(2)}, u32[]{:S(2)}) async-start(f32[8,8,32,128]{3,2,1,0:T(8,128)} %shard_map.75), calls=%async_computation.1 | async-start | bytes 2097152 | tf_op jit(solution)/shard_map/all_to_all | solution.py:71
  53.2 6.3 %copy-start.3 = (s32[256]{0:T(256)S(1)}, s32[256]{0:T(256)}, u32[]{:S(2)}) copy-start(s32[256]{0:T(256)} %param.7) | copy-start | bytes 3076
  53.2 53.8 %all-to-all-start.2 = ((f32[8,32,32,128]{3,2,1,0:T(8,128)}), f32[8,32,32,128]{3,2,1,0:T(8,128)}, u32[]{:S(2)}, u32[]{:S(2)}) async-start(f32[8,32,32,128]{3,2,1,0:T(8,128)} %bitcast.35), calls=%async_computation.2 | async-start | bytes 8388608 | tf_op jit(solution)/shard_map/all_to_all | solution.py:68
  57.9 113.5 %all-gather.2.cloned.1.call-start = ((), (), s32[]{:S(2)}) async-start(), calls=%async_computation.4 | async-start | bytes 5242880 | tf_op jit(solution)/shard_map/all_gather | solution.py:224
  112.9 53.7 %all-to-all-start.3 = ((f32[8,32,32,128]{3,2,1,0:T(8,128)}), f32[8,32,32,128]{3,2,1,0:T(8,128)}, u32[]{:S(2)}, u32[]{:S(2)}) async-start(f32[8,32,32,128]{3,2,1,0:T(8,128)} %shard_map.78), calls=%async_computation.3 | async-start | bytes 8388608 | tf_op jit(solution)/shard_map/all_to_all | solution.py:71
  189.9 48.1 %copy-start.2 = (f32[8,32,256]{2,1,0:T(8,128)S(1)}, f32[8,32,256]{2,1,0:T(8,128)}, u32[]{:S(2)}) copy-start(f32[8,32,256]{2,1,0:T(8,128)} %shard_map.79) | copy-start | bytes 786436
  238.0 8.3 %copy-start = (f32[256,4096]{1,0:T(8,128)S(1)}, f32[256,4096]{1,0:T(8,128)}, u32[]{:S(2)}) copy-start(f32[256,4096]{1,0:T(8,128)} %all-gather.2.cloned.1.call-done) | copy-start | bytes 12582916
Sparse Core Ops, SparseCore 0:
  60.9 82.3 all-gather.1

commit v3 on v2

--- a/solution.py
+++ b/solution.py
@@ -12,64 +12,252 @@
 MESH = pl.DeviceIdType.MESH
 
 
-def roll_kernel(n, count, blocks, shift_ref, in_hbm, out_ref, ring, sems):
-    copies = []
-    for i in range(n + 1):
-        copies.append(
-            pltpu.make_async_copy(
-                in_hbm.at[i % n], ring.at[:, pl.ds(i * blocks, blocks)], sems.at[i]
-            )
-        )
-    for copy in copies:
-        copy.start()
-    for copy in copies:
-        copy.wait()
+def roll_rows(n, blocks, first, count, shift_ref, ring, moved):
     total = n * blocks
 
     def one(k, carry):
-        shift = shift_ref[k]
+        shift = shift_ref[first + k]
+        ring[k, pl.ds(total, blocks), :] = ring[k, pl.ds(0, blocks), :]
         for j in range(n):
             start = lax.rem(j * blocks - shift + total, total)
-            out_ref[j, k] = ring[k, pl.ds(start, blocks), :]
+            moved[j, first + k] = ring[k, pl.ds(start, blocks), :]
         return carry
 
     lax.fori_loop(0, count, one, 0)
 
 
-def roll_rows(whole, shifts):
-    n, count, blocks, _ = whole.shape
+def exchange_kernel(
+    n,
+    depth,
+    pieces,
+    chunks,
+    panel_shift,
+    trail_shift,
+    panel,
+    trail,
+    full,
+    moved_t,
+    ring_p,
+    moved_p,
+    p1_send,
+    p1_recv,
+    t1_send,
+    t1_recv,
+    p2_send,
+    p2_recv,
+    z_send,
+    z_recv,
+    local_sem,
+    *rings,
+):
+    me = lax.axis_index("rows")
+    z = lax.axis_index("cols")
+    kp, blocks = panel.shape[1], panel.shape[2]
+    kt = trail.shape[1]
+    part = kt // chunks
+    width = n // pieces * kp
+    mine = pl.ds(pl.multiple_of(me * blocks, blocks), blocks)
+    place = pl.ds(me * kp, kp)
+
+    barrier = pltpu.get_barrier_semaphore()
+    for d in range(1, n):
+        pl.semaphore_signal(
+            barrier, inc=1, device_id={"rows": lax.rem(me + d, n)}, device_id_type=MESH
+        )
+
+    @pl.when(z > 0)
+    def _():
+        pl.semaphore_signal(barrier, inc=1, device_id={"cols": z - 1}, device_id_type=MESH)
+
+    @pl.when(z < depth - 1)
+    def _():
+        pl.semaphore_signal(barrier, inc=1, device_id={"cols": z + 1}, device_id_type=MESH)
+
+    sides = jnp.where(z > 0, 1, 0) + jnp.where(z < depth - 1, 1, 0)
+    pl.semaphore_wait(barrier, n - 1 + sides)
+
+    def row_copy(src, dst, send, recv, to):
+        return pltpu.make_async_remote_copy(
+            src_ref=src,
+            dst_ref=dst,
+            send_sem=send,
+            recv_sem=recv,
+            device_id={"rows": to},
+            device_id_type=MESH,
+        )
+
+    far = [lax.rem(me + d, n) for d in range(1, n)]
+    p1 = [
+        row_copy(panel.at[to], ring_p.at[:, mine], p1_send.at[i], p1_recv.at[i], to)
+        for i, to in enumerate(far)
+    ]
+    own_p1 = pltpu.make_async_copy(panel.at[me], ring_p.at[:, mine], local_sem.at[0])
+    t1, own_t1 = [], []
+    for c in range(chunks):
+        span = pl.ds(c * part, part)
+        t1.append(
+            [
+                row_copy(
+                    trail.at[to, span],
+                    rings[c].at[:, mine],
+                    t1_send.at[c, i],
+                    t1_recv.at[c, i],
+                    to,
+                )
+                for i, to in enumerate(far)
+            ]
+        )
+        own_t1.append(
+            pltpu.make_async_copy(
+                trail.at[me, span], rings[c].at[:, mine], local_sem.at[2 + c]
+            )
+        )
+    p2 = [
+        row_copy(moved_p.at[to], full.at[z, place], p2_send.at[i], p2_recv.at[i], to)
+        for i, to in enumerate(far)
+    ]
+    own_p2 = pltpu.make_async_copy(moved_p.at[me], full.at[z, place], local_sem.at[1])
+
+    def line(side, d, q):
+        step = 1 if side == 0 else -1
+        origin = z - step * (d - 1)
+        rows = pl.ds(q * width, width)
+        return pltpu.make_async_remote_copy(
+            src_ref=full.at[origin, rows],
+            dst_ref=full.at[origin, rows],
+            send_sem=z_send.at[side, d - 1, q],
+            recv_sem=z_recv.at[side, d - 1, q],
+            device_id={"cols": z + step},
+            device_id_type=MESH,
+        )
+
+    def sends(side, d):
+        if side == 0:
+            return (z + 1 < depth) & (z - (d - 1) >= 0)
+        return (z >= 1) & (z + (d - 1) < depth)
+
+    def receives(side, d):
+        return z - d >= 0 if side == 0 else z + d < depth
+
+    def arrived(side, d, q):
+        step = 1 if side == 0 else -1
+        origin = z - step * d
+        rows = pl.ds(q * width, width)
+        return pltpu.make_async_remote_copy(
+            src_ref=full.at[origin, rows],
+            dst_ref=full.at[origin, rows],
+            send_sem=z_send.at[side, d - 1, q],
+            recv_sem=z_recv.at[side, d - 1, q],
+            device_id={"cols": z - step},
+            device_id_type=MESH,
+        )
+
+    own_p1.start()
+    for copy in p1:
+        copy.start()
+    own_t1[0].start()
+    for copy in t1[0]:
+        copy.start()
+    own_p1.wait()
+    for copy in p1:
+        copy.wait_recv()
+    roll_rows(n, blocks, 0, kp, panel_shift, ring_p, moved_p)
+    own_p2.start()
+    for copy in p2:
+        copy.start()
+    for c in range(1, chunks):
+        own_t1[c].start()
+        for copy in t1[c]:
+            copy.start()
+    own_p2.wait()
+    for copy in p2:
+        copy.wait_recv()
+    for q in range(pieces):
+        for side in (0, 1):
+
+            @pl.when(sends(side, 1))
+            def _():
+                line(side, 1, q).start()
+
+    for c in range(chunks):
+        if c == chunks - 1:
+            for d in range(1, depth):
+                for q in range(pieces):
+                    for side in (0, 1):
+
+                        @pl.when(receives(side, d))
+                        def _():
+                            arrived(side, d, q).wait_recv()
+
+                        if d + 1 < depth:
+
+                            @pl.when(sends(side, d + 1))
+                            def _():
+                                line(side, d + 1, q).start()
+
+        own_t1[c].wait()
+        for copy in t1[c]:
+            copy.wait_recv()
+        roll_rows(n, blocks, c * part, part, trail_shift, rings[c], moved_t)
+    for copy in p1 + p2 + sum(t1, []):
+        copy.wait_send()
+    for d in range(1, depth):
+        for q in range(pieces):
+            for side in (0, 1):
+
+                @pl.when(sends(side, d))
+                def _():
+                    line(side, d, q).wait_send()
+
+
+def exchange(panel, trail, panel_shift, trail_shift, n, depth):
+    _, kp, blocks, _ = panel.shape
+    kt = trail.shape[1]
+    pieces = 4 if n % 4 == 0 else 1
+    chunks = 2 if kt % 2 == 0 else 1
+    f32 = jnp.float32
+    smem = pl.BlockSpec(memory_space=pltpu.SMEM)
+    vmem = pl.BlockSpec(memory_space=pltpu.VMEM)
+    hbm = pl.BlockSpec(memory_space=pl.ANY)
+    dma = pltpu.SemaphoreType.DMA
     return pl.pallas_call(
-        functools.partial(roll_kernel, n, count, blocks),
-        out_shape=jax.ShapeDtypeStruct(whole.shape, whole.dtype),
-        in_specs=[
-            pl.BlockSpec(memory_space=pltpu.SMEM),
-            pl.BlockSpec(memory_space=pl.ANY),
-        ],
-        out_specs=pl.BlockSpec(memory_space=pltpu.VMEM),
+        functools.partial(exchange_kernel, n, depth, pieces, chunks),
+        out_shape=(
+            jax.ShapeDtypeStruct((depth, n * kp, blocks, BW), f32),
+            jax.ShapeDtypeStruct(trail.shape, f32),
+        ),
+        in_specs=[smem, smem, hbm, hbm],
+        out_specs=(vmem, vmem),
         scratch_shapes=[
-            pltpu.VMEM((count, (n + 1) * blocks, BW), jnp.float32),
-            pltpu.SemaphoreType.DMA((n + 1,)),
-        ],
+            pltpu.VMEM((kp, (n + 1) * blocks, BW), f32),
+            pltpu.VMEM((n, kp, blocks, BW), f32),
+            dma((n - 1,)),
+            dma((n - 1,)),
+            dma((chunks, n - 1)),
+            dma((chunks, n - 1)),
+            dma((n - 1,)),
+            dma((n - 1,)),
+            dma((2, max(depth - 1, 1), pieces)),
+            dma((2, max(depth - 1, 1), pieces)),
+            dma((2 + chunks,)),
+        ]
+        + [pltpu.VMEM((kt // chunks, (n + 1) * blocks, BW), f32)] * chunks,
+        compiler_params=pltpu.CompilerParams(collective_id=3, has_side_effects=True),
         cost_estimate=pl.CostEstimate(
-            flops=0, bytes_accessed=2 * whole.size * 4, transcendentals=0
+            flops=0, bytes_accessed=40 * trail.size * 4, transcendentals=0
         ),
-    )(shifts, whole)
-
-
-def register(raw, shifts, n, my_row):
+    )(panel_shift, trail_shift, panel, trail)
+
+
+def grouped(raw, shifts, n, my_row):
     rows, pixels = raw.shape
-    blocks = pixels // BW
     padded = -(-rows // n) * n
     if padded != rows:
         raw = jnp.pad(raw, ((0, padded - rows), (0, 0)))
         shifts = jnp.pad(shifts, (0, padded - rows))
     count = padded // n
-    outgoing = raw.reshape(n, count, blocks, BW)
-    whole = lax.all_to_all(outgoing, "rows", split_axis=0, concat_axis=0, tiled=True)
     mine = lax.dynamic_slice_in_dim(shifts, my_row * count, count, 0)
-    moved = roll_rows(whole, mine)
-    back = lax.all_to_all(moved, "rows", split_axis=0, concat_axis=0, tiled=True)
-    return back.reshape(padded, pixels)[:rows]
+    return raw.reshape(n, count, pixels // BW, BW), mine
 
 
 def inner_rows(left, right, precision):
@@ -219,9 +407,14 @@
     n = lax.axis_size("rows")
     my_row = lax.axis_index("rows")
     root = math.sqrt(pixels * n)
-    reg_panel = register(raw_panel, panel_shift, n, my_row)
-    reg_trail = register(raw_trail, trail_shift, n, my_row)
-    full_panel = lax.all_gather(reg_panel, "cols", axis=0, tiled=True)
+    depth = lax.axis_size("cols")
+    trows = raw_trail.shape[0]
+    panel, panel_mine = grouped(raw_panel, panel_shift, n, my_row)
+    trail, trail_mine = grouped(raw_trail, trail_shift, n, my_row)
+    full, moved = exchange(panel, trail, panel_mine, trail_mine, n, depth)
+    full_panel = full.reshape(depth, -1, pixels)[:, :pcols].reshape(depth * pcols, pixels)
+    back = lax.all_to_all(moved, "rows", split_axis=0, concat_axis=0, tiled=True)
+    reg_trail = back.reshape(-1, pixels)[:trows]
     gram = sum_rows(inner_rows(full_panel, full_panel, lax.Precision.HIGHEST), n, 1)
     r_factor, inverse = factor(gram, 1.0 / root)
     cross = sum_rows(inner_rows(full_panel, reg_trail, lax.Precision.HIGH), n, 2)

time: 262 us -> 267 us (1.019)
  Pallas kernels: 61.7 us -> 201 us
  waiting for transfers between devices: 121 us -> 0.01 us
  between operations: 14.1 us -> 0.69 us
  starting transfers between devices: 18.1 us -> 6.08 us
  local copies, waits for them, and re-layouts: 16 us -> 23.4 us
  matrix products: 30.6 us -> 35.1 us
    all_to_all x4 -> x1, waiting for transfers between devices: 121 us -> 0.01 us  [on_device(): lax.all_to_all(moved, 'rows', split_axis=0, concat_axis=0, tiled=True)]
    pallas_call x2 -> x1, Pallas kernels: 9.06 us -> 121 us  [exchange(): pl.pallas_call(functools.partial(exchange_kernel, n, depth, pieces, chunk...]
    pallas_call x2, Pallas kernels: 25.5 us -> 52.6 us  [sum_rows(): pl.pallas_call(functools.partial(sum_kernel, n), out_shape=jax.ShapeDtype...]
    all_to_all x4 -> x1, starting transfers between devices: 18 us -> 6.08 us  [on_device(): lax.all_to_all(moved, 'rows', split_axis=0, concat_axis=0, tiled=True)]
    another operation x0 -> x1, local copies, waits for them, and re-layouts: none -> 4.95 us  [on_device(): full.reshape(depth, -1, pixels)[:, :pcols].reshape(depth * pcols, pixels)]
    dot_general x0 -> x1, local copies, waits for them, and re-layouts: none -> 4.94 us  [inner_rows(): lax.dot_general(left, right, (((1,), (1,)), ((), ())), precision=precisio...]
    dot_general x1, matrix products: 8.47 us -> 11.8 us  [on_device(): lax.dot_general(weights, full_panel, (((0,), (0,)), ((), ())), precision=...]
    unnamed x13 -> x8, local copies, waits for them, and re-layouts: 9.9 us -> 7.37 us
  transfers between devices with their start and end apart: 5 -> 1, of which waited for: 4 -> 0; matrix products, arithmetic and copies ran while one was open for 5% -> 9% of each run, Pallas kernels for 2% -> 25%
where the time goes in v3:
time: 267 us; the launch traced here: 266 us
  Pallas kernels  201 us (75%)
  matrix products  35.1 us (13%)
  local copies, waits for them, and re-layouts  23.4 us (9%)
  starting transfers between devices  6.08 us (2%)
    pallas_call x1, Pallas kernels, exchange(): pl.pallas_call(functools.partial(exchange_kernel, n, depth, pieces, chunk...  121 us
    pallas_call x2, Pallas kernels, sum_rows(): pl.pallas_call(functools.partial(sum_kernel, n), out_shape=jax.ShapeDtype...  52.6 us
    pallas_call x1, Pallas kernels, factor(): pl.pallas_call(functools.partial(factor_kernel, size, tile, scale), out_s...  26.9 us
    dot_general x2, matrix products, inner_rows(): lax.dot_general(left, right, (((1,), (1,)), ((), ())), precision=precisio...  13.8 us
    dot_general x1, matrix products, on_device(): lax.dot_general(weights, full_panel, (((0,), (0,)), ((), ())), precision=...  11.8 us
    unnamed x8, local copies, waits for them, and re-layouts  7.37 us
    dot_general x1, matrix products, on_device(): jnp.dot(own * root, full_panel, precision=lax.Precision.HIGH, preferred_e...  6.92 us
    all_to_all x1, starting transfers between devices, on_device(): lax.all_to_all(moved, 'rows', split_axis=0, concat_axis=0, tiled=True)  6.08 us
  transfers between devices with their start and end apart: 1, of which 0 were waited for; matrix products, arithmetic and copies ran while one was open for 9% of the time, Pallas kernels for 25%

profile of v3, /device:TPU:0, one launch (start us, length us, event | category | flops | bytes accessed | tf_op | source)
XLA Modules:
  0.0 266.3 jit_solution(15475912312781389794)
XLA Ops:
  0.6 2.4 copy.22
  3.0 0.0 copy-start.1
  3.0 0.0 copy-start.2
  3.0 5.0 %copy.9 = f32[32,8,32,128]{3,2,1,0:T(8,128)} copy(f32[32,8,32,128]{3,1,2,0:T(8,128)} %bitcast.39) | data formatting | bytes 8388608
  8.0 0.0 copy-done.1
  8.0 0.6 dynamic_slice.10.trail_shift
  8.6 0.0 copy-done.2
  8.6 0.6 dynamic_slice.9.panel_shift
  9.2 121.5 %shard_map.75 = (f32[4,64,32,128]{3,2,1,0:T(8,128)}, f32[8,32,32,128]{3,2,1,0:T(8,128)}) custom-call(s32[8]{0:T(128)} %dynamic_slice.9.panel_shift, s32[32]{0:T(128)} %dynamic_slice.10.trail_shift, f32[8,8,32,128]{3,2,1,0:T(8,128)} %copy.22, f32[8,32,32,128]{3,2,1,0:T(8,128)} %bitcast.38), custom_call_target="tpu_custom_call" | custom-call | bytes 167772160 | tf_op jit(solution)/shard_map/pallas_call | solution.py:223
  130.7 6.1 %all-to-all-start = ((f32[8,32,32,128]{3,2,1,0:T(8,128)}), f32[8,32,32,128]{3,2,1,0:T(8,128)}, u32[]{:S(2)}, u32[]{:S(2)}) async-start(f32[8,32,32,128]{3,2,1,0:T(8,128)} %get-tuple-element.11), calls=%async_computation | async-start | bytes 8388608 | tf_op jit(solution)/shard_map/all_to_all | solution.py:416
  136.8 4.9 %dot_general.20 = f32[8,32,4096]{2,1,0:T(8,128)} reshape(f32[4,64,32,128]{3,2,1,0:T(8,128)} %get-tuple-element.8) | data formatting | bytes 8388608 | tf_op jit(solution)/shard_map/dot_general | solution.py:264
  141.7 4.9 %reshape.34 = f32[256,4096,1]{1,0,2:T(8,128)} reshape(f32[4,64,32,128]{3,2,1,0:T(8,128)} %get-tuple-element.8) | data formatting | bytes 8388608 | tf_op jit(solution)/shard_map/reshape;reshape | solution.py:415
  146.6 7.7 %fusion.10.part_ref = f32[8,32,256]{2,1,0:T(8,128)} fusion(f32[8,32,4096]{2,1,0:T(8,128)} %dot_general.20, f32[256,4096,1]{1,0,2:T(8,128)} %reshape.34), kind=kOutput, calls=%fused_computation.13 | convolution fusion | flops 3221225472 | bytes 8650752 | tf_op jit(solution)/shard_map/dot_general | solution.py:264
  154.3 39.5 %shard_map.76 = f32[8,32,256]{2,1,0:T(8,128)} custom-call(f32[8,32,256]{2,1,0:T(8,128)} %fusion.10.part_ref), custom_call_target="tpu_custom_call" | custom-call | bytes 4194304 | tf_op jit(solution)/shard_map/pallas_call | solution.py:323
  193.8 26.9 %shard_map.77 = (f32[256,256]{1,0:T(8,128)}, f32[256,256]{1,0:T(8,128)}) custom-call(f32[256,256]{1,0:T(8,128)} %bitcast.41), custom_call_target="tpu_custom_call" | custom-call | flops 33554432 | bytes 15728640 | tf_op jit(solution)/shard_map/pallas_call | solution.py:389
  220.7 6.9 %fusion = f32[64,4096]{1,0:T(8,128)} fusion(f32[32,8,32,128]{3,2,1,0:T(8,128)} %bitcast.36, f32[256,256]{1,0:T(8,128)} %get-tuple-element.10, s32[]{:T(128)S(6)} %select_n.11), kind=kOutput, calls=%fused_computation.1 | convolution fusion | flops 402669568 | bytes 5308420 | tf_op jit(solution)/shard_map/dot_general | solution.py:439
  227.6 0.0 all-to-all-done
  227.6 5.0 %reshape.35 = f32[256,4096,1]{1,0,2:T(8,128)} reshape(f32[8,32,32,128]{3,2,1,0:T(8,128)} %all-to-all-done) | data formatting | bytes 8388608 | tf_op jit(solution)/shard_map/reshape | solution.py:417
  232.6 0.0 copy-start
  232.6 6.1 %fusion.11.part_ref = f32[8,32,256]{2,1,0:T(8,128)} fusion(f32[8,32,4096]{2,1,0:T(8,128)} %dot_general.20, f32[256,4096,1]{1,0,2:T(8,128)} %reshape.35), kind=kOutput, calls=%fused_computation.14 | convolution fusion | flops 1610612736 | bytes 8650752 | tf_op jit(solution)/shard_map/dot_general | solution.py:264
  238.7 13.1 %shard_map.78 = f32[8,32,256]{2,1,0:T(8,128)} custom-call(f32[8,32,256]{2,1,0:T(8,128)} %fusion.11.part_ref), custom_call_target="tpu_custom_call" | custom-call | bytes 4194304 | tf_op jit(solution)/shard_map/pallas_call | solution.py:323
  251.9 0.0 copy-done
  251.9 2.0 broadcast_multiply_fusion
  253.9 0.6 fusion.12
  254.5 11.8 %convolution_subtract_fusion = f32[256,4096]{1,0:T(8,128)} fusion(f32[256,256]{1,0:T(8,128)S(1)} %fusion.12, f32[32,8,32,128]{3,2,1,0:T(8,128)} %bitcast.15, f32[32,8,32,128]{3,2,1,0:T(8,128)} %bitcast.37), kind=kOutput, calls=%fused_computation | convolution fusion | flops 1611661312 | bytes 12845056 | tf_op jit(solution)/shard_map/dot_general | solution.py:430
Async XLA Ops:
  3.0 5.0 %copy-start.1 = (s32[256]{0:T(256)S(1)}, s32[256]{0:T(256)}, u32[]{:S(2)}) copy-start(s32[256]{0:T(256)} %param.7) | copy-start | bytes 3076
  3.0 5.6 %copy-start.2 = (s32[64]{0:T(128)S(1)}, s32[64]{0:T(128)}, u32[]{:S(2)}) copy-start(s32[64]{0:T(128)} %param.6) | copy-start | bytes 772
  130.7 97.0 %all-to-all-start = ((f32[8,32,32,128]{3,2,1,0:T(8,128)}), f32[8,32,32,128]{3,2,1,0:T(8,128)}, u32[]{:S(2)}, u32[]{:S(2)}) async-start(f32[8,32,32,128]{3,2,1,0:T(8,128)} %get-tuple-element.11), calls=%async_computation | async-start | bytes 8388608 | tf_op jit(solution)/shard_map/all_to_all | solution.py:416
  232.6 19.3 %copy-start = (f32[256,256]{1,0:T(8,128)S(1)}, f32[256,256]{1,0:T(8,128)}, u32[]{:S(2)}) copy-start(f32[256,256]{1,0:T(8,128)} %get-tuple-element.10) | copy-start | bytes 786436

commit v4 on v3

--- a/solution.py
+++ b/solution.py
@@ -20,7 +20,7 @@
         ring[k, pl.ds(total, blocks), :] = ring[k, pl.ds(0, blocks), :]
         for j in range(n):
             start = lax.rem(j * blocks - shift + total, total)
-            moved[j, first + k] = ring[k, pl.ds(start, blocks), :]
+            moved[j, k] = ring[k, pl.ds(start, blocks), :]
         return carry
 
     lax.fori_loop(0, count, one, 0)
@@ -36,15 +36,19 @@
     panel,
     trail,
     full,
-    moved_t,
+    back,
+    moved_b,
     ring_p,
     moved_p,
+    moved_a,
     p1_send,
     p1_recv,
     t1_send,
     t1_recv,
     p2_send,
     p2_recv,
+    t2_send,
+    t2_recv,
     z_send,
     z_recv,
     local_sem,
@@ -116,6 +120,11 @@
         row_copy(moved_p.at[to], full.at[z, place], p2_send.at[i], p2_recv.at[i], to)
         for i, to in enumerate(far)
     ]
+    t2 = [
+        row_copy(moved_a.at[to], back.at[me], t2_send.at[i], t2_recv.at[i], to)
+        for i, to in enumerate(far)
+    ]
+    own_t2 = pltpu.make_async_copy(moved_a.at[me], back.at[me], local_sem.at[2 + chunks])
     own_p2 = pltpu.make_async_copy(moved_p.at[me], full.at[z, place], local_sem.at[1])
 
     def line(side, d, q):
@@ -152,11 +161,22 @@
             device_id_type=MESH,
         )
 
+    def forward(d):
+        for q in range(pieces):
+            for side in (0, 1):
+
+                @pl.when(receives(side, d))
+                def _():
+                    arrived(side, d, q).wait_recv()
+
+                if d + 1 < depth:
+
+                    @pl.when(sends(side, d + 1))
+                    def _():
+                        line(side, d + 1, q).start()
+
     own_p1.start()
     for copy in p1:
-        copy.start()
-    own_t1[0].start()
-    for copy in t1[0]:
         copy.start()
     own_p1.wait()
     for copy in p1:
@@ -165,7 +185,7 @@
     own_p2.start()
     for copy in p2:
         copy.start()
-    for c in range(1, chunks):
+    for c in range(chunks):
         own_t1[c].start()
         for copy in t1[c]:
             copy.start()
@@ -179,27 +199,26 @@
             def _():
                 line(side, 1, q).start()
 
-    for c in range(chunks):
-        if c == chunks - 1:
-            for d in range(1, depth):
-                for q in range(pieces):
-                    for side in (0, 1):
-
-                        @pl.when(receives(side, d))
-                        def _():
-                            arrived(side, d, q).wait_recv()
-
-                        if d + 1 < depth:
-
-                            @pl.when(sends(side, d + 1))
-                            def _():
-                                line(side, d + 1, q).start()
-
-        own_t1[c].wait()
-        for copy in t1[c]:
-            copy.wait_recv()
-        roll_rows(n, blocks, c * part, part, trail_shift, rings[c], moved_t)
-    for copy in p1 + p2 + sum(t1, []):
+    forward(1)
+    own_t1[0].wait()
+    for copy in t1[0]:
+        copy.wait_recv()
+    roll_rows(n, blocks, 0, part, trail_shift, rings[0], moved_a)
+    own_t2.start()
+    for copy in t2:
+        copy.start()
+    if depth > 2:
+        forward(2)
+    own_t1[1].wait()
+    for copy in t1[1]:
+        copy.wait_recv()
+    roll_rows(n, blocks, part, part, trail_shift, rings[1], moved_b)
+    for d in range(3, depth):
+        forward(d)
+    own_t2.wait()
+    for copy in t2:
+        copy.wait_recv()
+    for copy in p1 + p2 + t1[0] + t1[1] + t2:
         copy.wait_send()
     for d in range(1, depth):
         for q in range(pieces):
@@ -214,7 +233,8 @@
     _, kp, blocks, _ = panel.shape
     kt = trail.shape[1]
     pieces = 4 if n % 4 == 0 else 1
-    chunks = 2 if kt % 2 == 0 else 1
+    chunks = 2
+    half = jax.ShapeDtypeStruct((n, kt // 2, blocks, BW), jnp.float32)
     f32 = jnp.float32
     smem = pl.BlockSpec(memory_space=pltpu.SMEM)
     vmem = pl.BlockSpec(memory_space=pltpu.VMEM)
@@ -224,22 +244,26 @@
         functools.partial(exchange_kernel, n, depth, pieces, chunks),
         out_shape=(
             jax.ShapeDtypeStruct((depth, n * kp, blocks, BW), f32),
-            jax.ShapeDtypeStruct(trail.shape, f32),
+            half,
+            half,
         ),
         in_specs=[smem, smem, hbm, hbm],
-        out_specs=(vmem, vmem),
+        out_specs=(vmem,) * 3,
         scratch_shapes=[
             pltpu.VMEM((kp, (n + 1) * blocks, BW), f32),
             pltpu.VMEM((n, kp, blocks, BW), f32),
+            pltpu.VMEM(half.shape, f32),
             dma((n - 1,)),
             dma((n - 1,)),
             dma((chunks, n - 1)),
             dma((chunks, n - 1)),
             dma((n - 1,)),
             dma((n - 1,)),
+            dma((n - 1,)),
+            dma((n - 1,)),
             dma((2, max(depth - 1, 1), pieces)),
             dma((2, max(depth - 1, 1), pieces)),
-            dma((2 + chunks,)),
+            dma((3 + chunks,)),
         ]
         + [pltpu.VMEM((kt // chunks, (n + 1) * blocks, BW), f32)] * chunks,
         compiler_params=pltpu.CompilerParams(collective_id=3, has_side_effects=True),
@@ -249,9 +273,9 @@
     )(panel_shift, trail_shift, panel, trail)
 
 
-def grouped(raw, shifts, n, my_row):
+def grouped(raw, shifts, n, my_row, unit):
     rows, pixels = raw.shape
-    padded = -(-rows // n) * n
+    padded = -(-rows // (n * unit)) * n * unit
     if padded != rows:
         raw = jnp.pad(raw, ((0, padded - rows), (0, 0)))
         shifts = jnp.pad(shifts, (0, padded - rows))
@@ -409,12 +433,14 @@
     root = math.sqrt(pixels * n)
     depth = lax.axis_size("cols")
     trows = raw_trail.shape[0]
-    panel, panel_mine = grouped(raw_panel, panel_shift, n, my_row)
-    trail, trail_mine = grouped(raw_trail, trail_shift, n, my_row)
-    full, moved = exchange(panel, trail, panel_mine, trail_mine, n, depth)
+    panel, panel_mine = grouped(raw_panel, panel_shift, n, my_row, 1)
+    trail, trail_mine = grouped(raw_trail, trail_shift, n, my_row, 2)
+    full, front, moved = exchange(panel, trail, panel_mine, trail_mine, n, depth)
     full_panel = full.reshape(depth, -1, pixels)[:, :pcols].reshape(depth * pcols, pixels)
-    back = lax.all_to_all(moved, "rows", split_axis=0, concat_axis=0, tiled=True)
-    reg_trail = back.reshape(-1, pixels)[:trows]
+    full_panel = lax.optimization_barrier(full_panel)
+    rest = lax.all_to_all(moved, "rows", split_axis=0, concat_axis=0, tiled=True)
+    reg_trail = jnp.concatenate([front, rest], axis=1).reshape(-1, pixels)[:trows]
+    reg_trail = lax.optimization_barrier(reg_trail)
     gram = sum_rows(inner_rows(full_panel, full_panel, lax.Precision.HIGHEST), n, 1)
     r_factor, inverse = factor(gram, 1.0 / root)
     cross = sum_rows(inner_rows(full_panel, reg_trail, lax.Precision.HIGH), n, 2)

time: 267 us -> 214 us (0.80)
  Pallas kernels: 201 us -> 165 us
  matrix products: 35.1 us -> 21.9 us
  local copies, waits for them, and re-layouts: 23.4 us -> 18.4 us
    pallas_call x1, Pallas kernels: 121 us -> 100 us  [exchange(): pl.pallas_call(functools.partial(exchange_kernel, n, depth, pieces, chunk...]
    pallas_call x2, Pallas kernels: 52.6 us -> 37.1 us  [sum_rows(): pl.pallas_call(functools.partial(sum_kernel, n), out_shape=jax.ShapeDtype...]
    unnamed x8 -> x16, local copies, waits for them, and re-layouts: 7.37 us -> 17.2 us
    dot_general x2, matrix products: 13.8 us -> 6.88 us  [inner_rows(): lax.dot_general(left, right, (((1,), (1,)), ((), ())), precision=precisio...]
    reshape x1 -> x0, local copies, waits for them, and re-layouts: 4.97 us -> none  [on_device(): reg_trail = back.reshape(-1, pixels)[:trows]]
    another operation x1 -> x0, local copies, waits for them, and re-layouts: 4.95 us -> none  [on_device(): full.reshape(depth, -1, pixels)[:, :pcols].reshape(depth * pcols, pixels)]
    dot_general x1 -> x0, local copies, waits for them, and re-layouts: 4.94 us -> none  [inner_rows(): lax.dot_general(left, right, (((1,), (1,)), ((), ())), precision=precisio...]
    dot_general x1, matrix products: 11.8 us -> 7.56 us  [on_device(): lax.dot_general(weights, full_panel, (((0,), (0,)), ((), ())), precision=...]
  transfers between devices with their start and end apart: 1 -> 1, of which waited for: 0 -> 0; matrix products, arithmetic and copies ran while one was open for 9% -> 7% of each run, Pallas kernels for 25% -> 24%
where the time goes in v4:
time: 214 us; the launch traced here: 213 us
  Pallas kernels  165 us (77%)
  matrix products  21.9 us (10%)
  local copies, waits for them, and re-layouts  18.4 us (9%)
  starting transfers between devices  5.45 us (3%)
  other arithmetic  2.27 us (1%)
    pallas_call x1, Pallas kernels, exchange(): pl.pallas_call(functools.partial(exchange_kernel, n, depth, pieces, chunk...  100 us
    pallas_call x2, Pallas kernels, sum_rows(): pl.pallas_call(functools.partial(sum_kernel, n), out_shape=jax.ShapeDtype...  37.1 us
    pallas_call x1, Pallas kernels, factor(): pl.pallas_call(functools.partial(factor_kernel, size, tile, scale), out_s...  27.1 us
    unnamed x16, local copies, waits for them, and re-layouts  17.2 us
    dot_general x1, matrix products, on_device(): lax.dot_general(weights, full_panel, (((0,), (0,)), ((), ())), precision=...  7.56 us
    dot_general x2, matrix products, inner_rows(): lax.dot_general(left, right, (((1,), (1,)), ((), ())), precision=precisio...  6.88 us
    all_to_all x1, starting transfers between devices, on_device(): lax.all_to_all(moved, 'rows', split_axis=0, concat_axis=0, tiled=True)  5.45 us
    dot_general x1, matrix products, on_device(): jnp.dot(own * root, full_panel, precision=lax.Precision.HIGH, preferred_e...  4.59 us
  transfers between devices with their start and end apart: 1, of which 0 were waited for; matrix products, arithmetic and copies ran while one was open for 7% of the time, Pallas kernels for 24%

profile of v4, /device:TPU:0, one launch (start us, length us, event | category | flops | bytes accessed | tf_op | source)
XLA Modules:
  0.0 213.3 jit_solution(1137276442558142607)
XLA Ops:
  0.6 2.4 %copy.17 = f32[8,8,32,128]{3,2,1,0:T(8,128)} copy(f32[8,8,32,128]{3,1,2,0:T(8,128)} %bitcast.45) | data formatting | bytes 2097152
  3.0 0.0 copy-start.4
  3.0 0.0 copy-start.5
  3.0 5.0 %copy.9 = f32[32,8,32,128]{3,2,1,0:T(8,128)} copy(f32[32,8,32,128]{3,1,2,0:T(8,128)} %bitcast.41) | data formatting | bytes 8388608
  8.0 0.0 copy-done.4
  8.0 0.6 dynamic_slice.10.trail_shift
  8.6 0.0 copy-done.5
  8.6 0.6 dynamic_slice.9.panel_shift
  9.2 100.4 %shard_map.75 = (f32[4,64,32,128]{3,2,1,0:T(8,128)}, f32[8,16,32,128]{3,2,1,0:T(8,128)}, f32[8,16,32,128]{3,2,1,0:T(8,128)}) custom-call(s32[8]{0:T(128)} %dynamic_slice.9.panel_shift, s32[32]{0:T(128)} %dynamic_slice.10.trail_shift, f32[8,8,32,128]{3,2,1,0:T(8,128)} %copy.17, f32[8,32,32,128]{3,2,1,0:T(8,128)} %bitcast.39), custom_call_target="tpu_custom_call" | custom-call | bytes 167772160 | tf_op jit(solution)/shard_map/pallas_call | solution.py:243
  109.5 5.5 %all-to-all-start = ((f32[8,16,32,128]{3,2,1,0:T(8,128)}), f32[8,16,32,128]{3,2,1,0:T(8,128)S(1)}, u32[]{:S(2)}, u32[]{:S(2)}) async-start(f32[8,16,32,128]{3,2,1,0:T(8,128)} %get-tuple-element.13), calls=%async_computation | async-start | bytes 4194304 | tf_op jit(solution)/shard_map/all_to_all | solution.py:441
  115.0 6.0 %copy.16 = f32[32,8,32,128]{3,1,2,0:T(8,128)S(1)} copy(f32[32,8,32,128]{3,2,1,0:T(8,128)} %bitcast.42) | data formatting | bytes 8388608
  121.0 0.0 copy-start
  121.0 4.2 %fusion.6 = f32[256,256]{1,0:T(8,128)} fusion(f32[256,4096]{1,0:T(8,128)S(1)} %bitcast.33), kind=kOutput, calls=%fused_computation.12 | convolution fusion | flops 3221225472 | bytes 4456448 | tf_op jit(solution)/shard_map/dot_general | solution.py:288
  125.2 0.0 copy-done
  125.2 24.3 %shard_map.76 = f32[8,32,256]{2,1,0:T(8,128)} custom-call(f32[8,32,256]{2,1,0:T(8,128)} %bitcast.43), custom_call_target="tpu_custom_call" | custom-call | bytes 4194304 | tf_op jit(solution)/shard_map/pallas_call | solution.py:347
  149.5 27.1 %shard_map.77 = (f32[256,256]{1,0:T(8,128)}, f32[256,256]{1,0:T(8,128)}) custom-call(f32[256,256]{1,0:T(8,128)} %bitcast.46), custom_call_target="tpu_custom_call" | custom-call | flops 33554432 | bytes 15728640 | tf_op jit(solution)/shard_map/pallas_call | solution.py:413
  176.6 4.6 %fusion = f32[64,4096]{1,0:T(8,128)} fusion(f32[256,4096]{1,0:T(8,128)} %bitcast.34, f32[256,256]{1,0:T(8,128)} %get-tuple-element.11, s32[]{:T(128)S(6)} %select_n.11), kind=kOutput, calls=%fused_computation.6 | convolution fusion | flops 402669568 | bytes 5308420 | tf_op jit(solution)/shard_map/dot_general | solution.py:465
  181.2 0.0 all-to-all-done
  181.2 2.3 %pad_maximum_fusion = f32[8,32,32,128]{3,2,1,0:T(8,128)S(1)} fusion(f32[8,16,32,128]{3,2,1,0:T(8,128)S(1)} %all-to-all-done, f32[8,16,32,128]{3,2,1,0:T(8,128)} %get-tuple-element.12), kind=kLoop, calls=%fused_computation.3 | loop fusion | flops 1048576 | bytes 8388608 | tf_op jit(solution)/shard_map/concatenate | solution.py:442
  183.5 0.0 copy-start.1
  183.5 3.9 %copy.15 = f32[32,8,32,128]{3,1,2,0:T(8,128)S(1)} copy(f32[32,8,32,128]{3,2,1,0:T(8,128)S(1)} %bitcast.40) | data formatting | bytes 8388608
  187.3 0.0 copy-start.2
  187.4 0.0 copy-done.1
  187.4 0.0 copy-start.3
  187.4 2.6 %fusion.7 = f32[256,256]{1,0:T(8,128)} fusion(f32[256,4096]{1,0:T(8,128)S(1)} %bitcast.36, f32[256,4096]{1,0:T(8,128)S(1)} %bitcast.37), kind=kOutput, calls=%fused_computation.13 | convolution fusion | flops 1610612736 | bytes 8650752 | tf_op jit(solution)/shard_map/dot_general | solution.py:288
  190.0 0.0 copy-done.2
  190.0 12.8 %shard_map.78 = f32[8,32,256]{2,1,0:T(8,128)} custom-call(f32[8,32,256]{2,1,0:T(8,128)} %bitcast.44), custom_call_target="tpu_custom_call" | custom-call | bytes 4194304 | tf_op jit(solution)/shard_map/pallas_call | solution.py:347
  202.8 0.0 copy-done.3
  202.9 2.0 broadcast_multiply_fusion
  204.9 0.8 fusion.8
  205.7 7.6 %convolution_subtract_fusion = f32[256,4096]{1,0:T(8,128)} fusion(f32[256,4096]{1,0:T(8,128)} %bitcast.38, f32[256,256]{1,0:T(8,128)S(1)} %fusion.8, f32[256,4096]{1,0:T(8,128)} %bitcast.35), kind=kOutput, calls=%fused_computation | convolution fusion | flops 1611661312 | bytes 12845056 | tf_op jit(solution)/shard_map/dot_general | solution.py:456
Async XLA Ops:
  3.0 5.0 %copy-start.4 = (s32[256]{0:T(256)S(1)}, s32[256]{0:T(256)}, u32[]{:S(2)}) copy-start(s32[256]{0:T(256)} %param.7) | copy-start | bytes 3076
  3.0 5.6 %copy-start.5 = (s32[64]{0:T(128)S(1)}, s32[64]{0:T(128)}, u32[]{:S(2)}) copy-start(s32[64]{0:T(128)} %param.6) | copy-start | bytes 772
  109.5 71.7 %all-to-all-start = ((f32[8,16,32,128]{3,2,1,0:T(8,128)}), f32[8,16,32,128]{3,2,1,0:T(8,128)S(1)}, u32[]{:S(2)}, u32[]{:S(2)}) async-start(f32[8,16,32,128]{3,2,1,0:T(8,128)} %get-tuple-element.13), calls=%async_computation | async-start | bytes 4194304 | tf_op jit(solution)/shard_map/all_to_all | solution.py:441
  121.0 4.3 %copy-start = (f32[32,8,32,128]{3,1,2,0:T(8,128)}, f32[32,8,32,128]{3,1,2,0:T(8,128)S(1)}, u32[]{:S(2)}) copy-start(f32[32,8,32,128]{3,1,2,0:T(8,128)S(1)} %copy.16) | copy-start | bytes 12582916
  183.5 3.9 %copy-start.1 = (f32[32,8,32,128]{3,1,2,0:T(8,128)S(1)}, f32[32,8,32,128]{3,1,2,0:T(8,128)}, u32[]{:S(2)}) copy-start(f32[32,8,32,128]{3,1,2,0:T(8,128)} %copy-done) | copy-start | bytes 12582916
  187.3 2.7 %copy-start.2 = (f32[32,8,32,128]{3,1,2,0:T(8,128)}, f32[32,8,32,128]{3,1,2,0:T(8,128)S(1)}, u32[]{:S(2)}) copy-start(f32[32,8,32,128]{3,1,2,0:T(8,128)S(1)} %copy.15) | copy-start | bytes 12582916
  187.4 15.5 %copy-start.3 = (f32[256,256]{1,0:T(8,128)S(1)}, f32[256,256]{1,0:T(8,128)}, u32[]{:S(2)}) copy-start(f32[256,256]{1,0:T(8,128)} %get-tuple-element.11) | copy-start | bytes 786436

commit v5 on v4

--- a/solution.py
+++ b/solution.py
@@ -438,10 +438,11 @@
     full, front, moved = exchange(panel, trail, panel_mine, trail_mine, n, depth)
     full_panel = full.reshape(depth, -1, pixels)[:, :pcols].reshape(depth * pcols, pixels)
     full_panel = lax.optimization_barrier(full_panel)
+    gram = sum_rows(inner_rows(full_panel, full_panel, lax.Precision.HIGHEST), n, 1)
+    gram, moved = lax.optimization_barrier((gram, moved))
     rest = lax.all_to_all(moved, "rows", split_axis=0, concat_axis=0, tiled=True)
     reg_trail = jnp.concatenate([front, rest], axis=1).reshape(-1, pixels)[:trows]
     reg_trail = lax.optimization_barrier(reg_trail)
-    gram = sum_rows(inner_rows(full_panel, full_panel, lax.Precision.HIGHEST), n, 1)
     r_factor, inverse = factor(gram, 1.0 / root)
     cross = sum_rows(inner_rows(full_panel, reg_trail, lax.Precision.HIGH), n, 2)
     highest = lax.Precision.HIGHEST

time: 214 us -> 204 us (0.953)
  Pallas kernels: 165 us -> 157 us
    pallas_call x2, Pallas kernels: 37.1 us -> 29.4 us  [sum_rows(): pl.pallas_call(functools.partial(sum_kernel, n), out_shape=jax.ShapeDtype...]
  transfers between devices with their start and end apart: 1 -> 1, of which waited for: 0 -> 0; matrix products, arithmetic and copies ran while one was open for 7% -> 2% of each run, Pallas kernels for 24% -> 13%
where the time goes in v5:
time: 204 us
  Pallas kernels  157 us (77%)
  matrix products  21.7 us (11%)
  local copies, waits for them, and re-layouts  18.6 us (9%)
  starting transfers between devices  3.79 us (2%)
  other arithmetic  2.27 us (1%)
    pallas_call x1, Pallas kernels, exchange(): pl.pallas_call(functools.partial(exchange_kernel, n, depth, pieces, chunk...  100 us
    pallas_call x2, Pallas kernels, sum_rows(): pl.pallas_call(functools.partial(sum_kernel, n), out_shape=jax.ShapeDtype...  29.4 us
    pallas_call x1, Pallas kernels, factor(): pl.pallas_call(functools.partial(factor_kernel, size, tile, scale), out_s...  26.9 us
    unnamed x16, local copies, waits for them, and re-layouts  17.4 us
    dot_general x1, matrix products, on_device(): lax.dot_general(weights, full_panel, (((0,), (0,)), ((), ())), precision=...  7.56 us
    dot_general x2, matrix products, inner_rows(): lax.dot_general(left, right, (((1,), (1,)), ((), ())), precision=precisio...  6.88 us
    dot_general x1, matrix products, on_device(): jnp.dot(own * root, full_panel, precision=lax.Precision.HIGH, preferred_e...  4.59 us
  transfers between devices with their start and end apart: 1, of which 0 were waited for; matrix products, arithmetic and copies ran while one was open for 2% of the time, Pallas kernels for 13%

profile of v5, /device:TPU:0, one launch (start us, length us, event | category | flops | bytes accessed | tf_op | source)
XLA Modules:
  0.0 203.7 jit_solution(7507506265094147585)
XLA Ops:
  0.6 2.4 %copy.17 = f32[8,8,32,128]{3,2,1,0:T(8,128)} copy(f32[8,8,32,128]{3,1,2,0:T(8,128)} %bitcast.45) | data formatting | bytes 2097152
  3.0 0.0 copy-start.4
  3.0 0.0 copy-start.5
  3.0 5.0 %copy.9 = f32[32,8,32,128]{3,2,1,0:T(8,128)} copy(f32[32,8,32,128]{3,1,2,0:T(8,128)} %bitcast.41) | data formatting | bytes 8388608
  8.0 0.0 copy-done.4
  8.0 0.6 dynamic_slice.10.trail_shift
  8.6 0.0 copy-done.5
  8.6 0.6 dynamic_slice.9.panel_shift
  9.2 100.4 %shard_map.75 = (f32[4,64,32,128]{3,2,1,0:T(8,128)}, f32[8,16,32,128]{3,2,1,0:T(8,128)}, f32[8,16,32,128]{3,2,1,0:T(8,128)}) custom-call(s32[8]{0:T(128)} %dynamic_slice.9.panel_shift, s32[32]{0:T(128)} %dynamic_slice.10.trail_shift, f32[8,8,32,128]{3,2,1,0:T(8,128)} %copy.17, f32[8,32,32,128]{3,2,1,0:T(8,128)} %bitcast.39), custom_call_target="tpu_custom_call" | custom-call | bytes 167772160 | tf_op jit(solution)/shard_map/pallas_call | solution.py:243
  109.5 6.0 %copy.16 = f32[32,8,32,128]{3,1,2,0:T(8,128)S(1)} copy(f32[32,8,32,128]{3,2,1,0:T(8,128)} %bitcast.42) | data formatting | bytes 8388608
  115.5 0.0 copy-start
  115.5 4.2 %fusion.6 = f32[256,256]{1,0:T(8,128)} fusion(f32[256,4096]{1,0:T(8,128)S(1)} %bitcast.33), kind=kOutput, calls=%fused_computation.12 | convolution fusion | flops 3221225472 | bytes 4456448 | tf_op jit(solution)/shard_map/dot_general | solution.py:288
  119.8 0.0 copy-done
  119.8 15.9 %shard_map.76 = f32[8,32,256]{2,1,0:T(8,128)} custom-call(f32[8,32,256]{2,1,0:T(8,128)} %bitcast.43), custom_call_target="tpu_custom_call" | custom-call | bytes 4194304 | tf_op jit(solution)/shard_map/pallas_call | solution.py:347
  135.7 3.8 %all-to-all-start = ((f32[8,16,32,128]{3,2,1,0:T(8,128)}), f32[8,16,32,128]{3,2,1,0:T(8,128)S(1)}, u32[]{:S(2)}, u32[]{:S(2)}) async-start(f32[8,16,32,128]{3,2,1,0:T(8,128)} %get-tuple-element.17), calls=%async_computation | async-start | bytes 4194304 | tf_op jit(solution)/shard_map/all_to_all | solution.py:443
  139.5 26.9 %shard_map.77 = (f32[256,256]{1,0:T(8,128)}, f32[256,256]{1,0:T(8,128)}) custom-call(f32[256,256]{1,0:T(8,128)} %bitcast.46), custom_call_target="tpu_custom_call" | custom-call | flops 33554432 | bytes 15728640 | tf_op jit(solution)/shard_map/pallas_call | solution.py:413
  166.4 4.6 %fusion = f32[64,4096]{1,0:T(8,128)} fusion(f32[256,4096]{1,0:T(8,128)} %bitcast.34, f32[256,256]{1,0:T(8,128)} %get-tuple-element.15, s32[]{:T(128)S(6)} %select_n.11), kind=kOutput, calls=%fused_computation.6 | convolution fusion | flops 402669568 | bytes 5308420 | tf_op jit(solution)/shard_map/dot_general | solution.py:466
  170.9 0.0 all-to-all-done
  170.9 2.3 %pad_maximum_fusion = f32[8,32,32,128]{3,2,1,0:T(8,128)S(1)} fusion(f32[8,16,32,128]{3,2,1,0:T(8,128)S(1)} %all-to-all-done, f32[8,16,32,128]{3,2,1,0:T(8,128)} %get-tuple-element.16), kind=kLoop, calls=%fused_computation.3 | loop fusion | flops 1048576 | bytes 8388608 | tf_op jit(solution)/shard_map/concatenate | solution.py:444
  173.2 0.0 copy-start.1
  173.2 4.1 %copy.15 = f32[32,8,32,128]{3,1,2,0:T(8,128)S(1)} copy(f32[32,8,32,128]{3,2,1,0:T(8,128)S(1)} %bitcast.40) | data formatting | bytes 8388608
  177.3 0.0 copy-start.2
  177.3 0.0 copy-done.1
  177.3 0.0 copy-start.3
  177.3 2.6 %fusion.7 = f32[256,256]{1,0:T(8,128)} fusion(f32[256,4096]{1,0:T(8,128)S(1)} %bitcast.36, f32[256,4096]{1,0:T(8,128)S(1)} %bitcast.37), kind=kOutput, calls=%fused_computation.13 | convolution fusion | flops 1610612736 | bytes 8650752 | tf_op jit(solution)/shard_map/dot_general | solution.py:288
  180.0 0.0 copy-done.2
  180.0 13.5 %shard_map.78 = f32[8,32,256]{2,1,0:T(8,128)} custom-call(f32[8,32,256]{2,1,0:T(8,128)} %bitcast.44), custom_call_target="tpu_custom_call" | custom-call | bytes 4194304 | tf_op jit(solution)/shard_map/pallas_call | solution.py:347
  193.5 0.0 copy-done.3
  193.5 2.0 broadcast_multiply_fusion
  195.6 0.6 fusion.8
  196.2 7.6 %convolution_subtract_fusion = f32[256,4096]{1,0:T(8,128)} fusion(f32[256,4096]{1,0:T(8,128)} %bitcast.38, f32[256,256]{1,0:T(8,128)S(1)} %fusion.8, f32[256,4096]{1,0:T(8,128)} %bitcast.35), kind=kOutput, calls=%fused_computation | convolution fusion | flops 1611661312 | bytes 12845056 | tf_op jit(solution)/shard_map/dot_general | solution.py:457
Async XLA Ops:
  3.0 5.0 %copy-start.4 = (s32[256]{0:T(256)S(1)}, s32[256]{0:T(256)}, u32[]{:S(2)}) copy-start(s32[256]{0:T(256)} %param.7) | copy-start | bytes 3076
  3.0 5.6 %copy-start.5 = (s32[64]{0:T(128)S(1)}, s32[64]{0:T(128)}, u32[]{:S(2)}) copy-start(s32[64]{0:T(128)} %param.6) | copy-start | bytes 772
  115.5 4.3 %copy-start = (f32[32,8,32,128]{3,1,2,0:T(8,128)}, f32[32,8,32,128]{3,1,2,0:T(8,128)S(1)}, u32[]{:S(2)}) copy-start(f32[32,8,32,128]{3,1,2,0:T(8,128)S(1)} %copy.16) | copy-start | bytes 12582916
  135.7 35.3 %all-to-all-start = ((f32[8,16,32,128]{3,2,1,0:T(8,128)}), f32[8,16,32,128]{3,2,1,0:T(8,128)S(1)}, u32[]{:S(2)}, u32[]{:S(2)}) async-start(f32[8,16,32,128]{3,2,1,0:T(8,128)} %get-tuple-element.17), calls=%async_computation | async-start | bytes 4194304 | tf_op jit(solution)/shard_map/all_to_all | solution.py:443
  173.2 4.1 %copy-start.1 = (f32[32,8,32,128]{3,1,2,0:T(8,128)S(1)}, f32[32,8,32,128]{3,1,2,0:T(8,128)}, u32[]{:S(2)}) copy-start(f32[32,8,32,128]{3,1,2,0:T(8,128)} %copy-done) | copy-start | bytes 12582916
  177.3 2.7 %copy-start.2 = (f32[32,8,32,128]{3,1,2,0:T(8,128)}, f32[32,8,32,128]{3,1,2,0:T(8,128)S(1)}, u32[]{:S(2)}) copy-start(f32[32,8,32,128]{3,1,2,0:T(8,128)S(1)} %copy.15) | copy-start | bytes 12582916
  177.3 16.2 %copy-start.3 = (f32[256,256]{1,0:T(8,128)S(1)}, f32[256,256]{1,0:T(8,128)}, u32[]{:S(2)}) copy-start(f32[256,256]{1,0:T(8,128)} %get-tuple-element.15) | copy-start | bytes 786436
